TPU v7x, 128 devices: a whole 4x4x4 slice. The times are simulated.
128 devices in a mesh: gx: 4 (over y), gy: 4 (over x_lo, core), gz: 8 (over x_hi, z).
Axes of the slice: x: 4 (x_hi: 2, x_lo: 2; x = x_hi * 2 + x_lo), y: 4, z: 4, core: 2. Of those that a mesh axis runs over, the one named last changes fastest.
Arguments:
- inputs: bfloat16 [112, 112, 56, 96], P('gx', 'gy', 'gz'), may hold values from -6 to 6
- d_out: bfloat16 [112, 112, 56, 96], P('gx', 'gy', 'gz'), may hold values from -6 to 6
- layer_norm_gain: float32 [96], replicated, may hold values from 0.1 to 1.9
- layer_norm_bias: float32 [96], replicated, may hold values from -3 to 3
- w_qkv: bfloat16 [96, 288], replicated, may hold values from -0.625 to 0.625
- b_qkv: float32 [288], replicated, may hold values from -3 to 3
- w_proj: bfloat16 [96, 96], replicated, may hold values from -0.625 to 0.625
- rel_bias: float32 [3, 2197], replicated, may hold values from -4 to 240
Outputs:
- d_x: bfloat16 [112, 112, 56, 96], P('gx', 'gy', 'gz')
- g_qkv: float32 [96, 288], replicated
- g_bqkv: float32 [288], replicated
- g_proj: float32 [96, 96], replicated
- g_rel: float32 [3, 2197], replicated
- gain_gradient: float32 [96], replicated
- g_shift: float32 [96], replicated
All inputs are finite; a program needn't handle non-finite values.
Results may differ from a plain program's by a relative error of at most 0.011.
Values may be sent and summed in bfloat16 or wider, within the bound.
A program may use at most 192 MiB of HBM per device.

v0:
```python
import jax
import jax.numpy as jnp
from jax import lax
from jax.sharding import PartitionSpec as P

WIN = 7
SHIFT = 3


def shifted(block, axis, distance):
    devices = range(lax.axis_size(axis))
    route = [((i - distance) % len(devices), i) for i in devices]
    return lax.ppermute(block, axis, route)


def in_one(arrays, axis):
    ends = [0]
    for a in arrays:
        ends.append(ends[-1] + a.size)
    so_far = lax.psum(jnp.concatenate([a.ravel() for a in arrays]), axis)
    return tuple((so_far[b:e].reshape(a.shape) for a, b, e in zip(arrays, ends, ends[1:])))


def offset_ones(span):
    first = jnp.arange(span)[:, None, None]
    second = jnp.arange(span)[None, :, None]
    third = jnp.arange(2 * span - 1)[None, None, :]
    return (first - second + span - 1 == third).astype(jnp.float32)


def expand_table(table, span):
    exact = lax.Precision.HIGHEST
    ones = offset_ones(span)
    width = 2 * span - 1
    heads = table.shape[0]
    cube = table.reshape(heads, width, width, width)
    section = jnp.einsum("hxyz,cCz->hxycC", cube, ones, precision=exact)
    section = jnp.einsum("hxycC,bBy->hxbcBC", section, ones, precision=exact)
    section = jnp.einsum("hxbcBC,aAx->habcABC", section, ones, precision=exact)
    return section.reshape(heads, span**3, span**3)


def fold_table(pairs, span):
    exact = lax.Precision.HIGHEST
    ones = offset_ones(span)
    heads = pairs.shape[0]
    grid = pairs.reshape(heads, span, span, span, span, span, span)
    section = jnp.einsum("habcABC,aAx->hxbcBC", grid, ones, precision=exact)
    section = jnp.einsum("hxbcBC,bBy->hxycC", section, ones, precision=exact)
    section = jnp.einsum("hxycC,cCz->hxyz", section, ones, precision=exact)
    return section.reshape(heads, -1)


def region_label(start, cells, count):
    places = start + jnp.arange(cells)
    return jnp.where(places < count - WIN, 0, jnp.where(places < count - SHIFT, 1, 2)).astype(
        jnp.int32
    )


def to_windows(array):
    first, second, third = array.shape[:3]
    rest = array.shape[3:]
    shaped = array.reshape((first // WIN, WIN, second // WIN, WIN, third // WIN, WIN) + rest)
    order = (0, 2, 4, 1, 3, 5) + tuple(range(6, 6 + len(rest)))
    return shaped.transpose(order).reshape((-1, WIN**3) + rest)


def from_windows(array, first, second, third):
    feats = array.shape[-1]
    shaped = array.reshape(first // WIN, second // WIN, third // WIN, WIN, WIN, WIN, feats)
    return shaped.transpose(0, 3, 1, 4, 2, 5, 6).reshape(first, second, third, feats)


def forward_depth(pair):
    arrived = shifted(pair[:, :SHIFT], "gx", -1)
    return jnp.concatenate([pair[:, SHIFT:], arrived], 1)


def forward_height(pair):
    arrived = shifted(pair[:, :, :SHIFT], "gy", -1)
    return jnp.concatenate([pair[:, :, SHIFT:], arrived], 2)


def forward_width(pair):
    arrived = shifted(pair[:, :, :, :SHIFT], "gz", -1)
    return jnp.concatenate([pair[:, :, :, SHIFT:], arrived], 3)


def backward_depth(field):
    edge = field.shape[0] - SHIFT
    arrived = shifted(field[edge:], "gx", 1)
    return jnp.concatenate([arrived, field[:edge]], 0)


def backward_height(field):
    edge = field.shape[1] - SHIFT
    arrived = shifted(field[:, edge:], "gy", 1)
    return jnp.concatenate([arrived, field[:, :edge]], 1)


def backward_width(field):
    edge = field.shape[2] - SHIFT
    arrived = shifted(field[:, :, edge:], "gz", 1)
    return jnp.concatenate([arrived, field[:, :, :edge]], 2)


def window_pass(ln_w, dy_w, lab_w, w_qkv, b_qkv, w_proj, bias_full):
    f32 = jnp.float32
    bf16 = jnp.bfloat16
    group, tok, feats = ln_w.shape
    heads = bias_full.shape[0]
    hdim = feats // heads
    scale = hdim ** (-0.5)
    qkv = jnp.einsum("gtc,cf->gtf", ln_w, w_qkv, preferred_element_type=f32) + b_qkv
    qkv = qkv.astype(bf16).reshape(group, tok, 3, heads, hdim)
    query = qkv[:, :, 0].transpose(0, 2, 1, 3)
    keys = qkv[:, :, 1].transpose(0, 2, 1, 3)
    values = qkv[:, :, 2].transpose(0, 2, 1, 3)
    scores = (
        jnp.einsum("ghid,ghjd->ghij", query, keys, preferred_element_type=f32) * scale
        + bias_full[None]
    )
    allowed = (lab_w[:, :, None] == lab_w[:, None, :])[:, None]
    scores = jnp.where(allowed, scores, f32(-1e30))
    top = jnp.max(scores, -1, keepdims=True)
    expo = jnp.exp(scores - top)
    probs = expo / jnp.sum(expo, -1, keepdims=True)
    probs_b = probs.astype(bf16)
    attended = jnp.einsum("ghij,ghjd->ghid", probs_b, values, preferred_element_type=f32)
    attended = attended.transpose(0, 2, 1, 3).reshape(group, tok, feats).astype(bf16)
    grad_att = jnp.einsum("gtc,fc->gtf", dy_w, w_proj, preferred_element_type=f32).astype(bf16)
    proj_part = jnp.einsum("gtf,gtc->fc", attended, dy_w, preferred_element_type=f32)
    grad_heads = grad_att.reshape(group, tok, heads, hdim).transpose(0, 2, 1, 3)
    grad_probs = jnp.einsum("ghid,ghjd->ghij", grad_heads, values, preferred_element_type=f32)
    grad_v = jnp.einsum("ghij,ghid->ghjd", probs_b, grad_heads, preferred_element_type=f32)
    grad_scores = probs * (grad_probs - jnp.sum(probs * grad_probs, -1, keepdims=True))
    rel_part = jnp.sum(grad_scores, 0)
    scores_b = grad_scores.astype(bf16)
    grad_q = jnp.einsum("ghij,ghjd->ghid", scores_b, keys, preferred_element_type=f32) * scale
    grad_k = jnp.einsum("ghij,ghid->ghjd", scores_b, query, preferred_element_type=f32) * scale
    grad_qkv = (
        jnp.stack([grad_q, grad_k, grad_v], 1)
        .transpose(0, 3, 1, 2, 4)
        .reshape(group, tok, 3 * feats)
    )
    bias_part = jnp.sum(grad_qkv, (0, 1))
    qkv_b = grad_qkv.astype(bf16)
    weight_part = jnp.einsum("gtc,gtf->cf", ln_w, qkv_b, preferred_element_type=f32)
    grad_in = jnp.einsum("gtf,cf->gtc", qkv_b, w_qkv, preferred_element_type=f32)
    return (grad_in, (weight_part, bias_part, proj_part, rel_part))


def shards(inputs, d_out, layer_norm_gain, layer_norm_bias, w_qkv, b_qkv, w_proj, rel_bias):
    f32 = jnp.float32
    cells_x, cells_y, cells_z, feats = inputs.shape
    tok = WIN**3
    heads = rel_bias.shape[0]
    xf = inputs.astype(f32)
    centered_input = xf - jnp.mean(xf, -1, keepdims=True)
    inverse_deviation = lax.rsqrt(
        jnp.mean(centered_input * centered_input, -1, keepdims=True) + 1e-05
    )
    normalized_input = centered_input * inverse_deviation
    normalized_tokens = (normalized_input * layer_norm_gain + layer_norm_bias).astype(jnp.bfloat16)
    moved_pair = jnp.stack([normalized_tokens, d_out])
    forward_steps = (forward_depth, forward_height, forward_width)
    backward_steps = (backward_depth, backward_height, backward_width)
    for advance in forward_steps:
        moved_pair = advance(moved_pair)
    label_x = region_label(lax.axis_index("gx") * cells_x, cells_x, cells_x * lax.axis_size("gx"))
    label_y = region_label(lax.axis_index("gy") * cells_y, cells_y, cells_y * lax.axis_size("gy"))
    label_z = region_label(lax.axis_index("gz") * cells_z, cells_z, cells_z * lax.axis_size("gz"))
    labels = label_x[:, None, None] * 9 + label_y[None, :, None] * 3 + label_z[None, None, :]
    bias_full = expand_table(rel_bias, WIN)
    group = cells_y // WIN * (cells_z // WIN)
    win_ln = to_windows(moved_pair[0]).reshape(-1, group, tok, feats)
    win_dy = to_windows(moved_pair[1]).reshape(-1, group, tok, feats)
    win_lab = to_windows(labels).reshape(-1, group, tok)

    def step(carry, item):
        grad_in, parts = window_pass(item[0], item[1], item[2], w_qkv, b_qkv, w_proj, bias_full)
        return (tuple((total + part for total, part in zip(carry, parts))), grad_in)

    start = (
        jnp.zeros((feats, 3 * feats), f32),
        jnp.zeros((3 * feats,), f32),
        jnp.zeros((feats, feats), f32),
        jnp.zeros((heads, tok, tok), f32),
    )
    sums, grad_win = lax.scan(step, start, (win_ln, win_dy, win_lab))
    normalized_output_gradient = from_windows(
        grad_win.reshape(-1, tok, feats), cells_x, cells_y, cells_z
    )
    for retreat in backward_steps:
        normalized_output_gradient = retreat(normalized_output_gradient)
    normalized_gradient = normalized_output_gradient * layer_norm_gain
    input_gradient_norm = inverse_deviation * (
        normalized_gradient
        - jnp.mean(normalized_gradient, -1, keepdims=True)
        - normalized_input * jnp.mean(normalized_gradient * normalized_input, -1, keepdims=True)
    )
    d_x = (d_out.astype(f32) + input_gradient_norm).astype(jnp.bfloat16)
    rel_local = fold_table(sums[3], WIN)
    local_gain = jnp.sum(normalized_output_gradient * normalized_input, (0, 1, 2))
    shift_local = jnp.sum(normalized_output_gradient, (0, 1, 2))
    totals = in_one(
        (sums[0], sums[1], sums[2], rel_local, local_gain, shift_local), ("gx", "gy", "gz")
    )
    count = (
        cells_x
        * cells_y
        * cells_z
        * lax.axis_size("gx")
        * lax.axis_size("gy")
        * lax.axis_size("gz")
    )
    inverse_width_factor = float(count) ** (-0.5)
    return (
        d_x,
        totals[0] * inverse_width_factor,
        totals[1] * inverse_width_factor,
        totals[2] * inverse_width_factor,
        totals[3] * inverse_width_factor,
        totals[4] * inverse_width_factor,
        totals[5] * inverse_width_factor,
    )


def solution(mesh):
    placed = (P("gx", "gy", "gz", None), P("gx", "gy", "gz", None), P(), P(), P(), P(), P(), P())
    return jax.shard_map(
        shards,
        mesh=mesh,
        in_specs=placed,
        out_specs=(P("gx", "gy", "gz", None), P(), P(), P(), P(), P(), P()),
        check_vma=False,
    )
```

profile of v0, /device:TPU:0, one launch (start us, length us, event | category | flops | bytes accessed | tf_op | source)
XLA Modules:
  0.0 692.3 jit_solution(11061455618265051562)
XLA Ops:
  7.2 2.4 convert_reduce_fusion
  15.1 3.2 collective-permute-start
  20.0 9.5 %convolution_bitcast_fusion.5 = f32[3,13,7,7,7,7]{1,2,5,3,0,4:T(8,128)S(1)} fusion(f32[3,13,13,7,7]{2,3,1,0,4:T(8,128)S(1)} %convolution_bitcast_fusion.7, s32[7,7]{0,1:T(8,128)S(1)} %subtract_add_fusion), kind=kOutput, calls=%fused_computation.96 | convolution fusion | flops 14608321 | bytes 474124 | tf_op jit(solution)/shard_map/hxycC,bBy->hxbcBC/dot_general | solution.py:38
  30.5 18.2 %collective-permute-start.1 = (bf16[2,28,3,7,96]{4,3,2,1,0:T(8,128)(2,1)S(1)}, bf16[2,28,3,7,96]{4,3,2,1,0:T(8,128)(2,1)S(1)}, u32[]{:S(2)}, u32[]{:S(2)}) collective-permute-start(bf16[2,28,3,7,96]{4,3,2,1,0:T(8,128)(2,1)S(1)} %pad_maximum_fusion.5), channel_id=1, source_target_pairs={{8,0},{16,8},{24,16},{0,24},{9,1},{17,9},{25,17},{1,25},{10,2},{18... | collective-permute-start | bytes 677384 | tf_op jit(solution)/shard_map/ppermute | solution.py:13
  49.5 3.9 collective-permute-done.1
  54.3 2.9 copy.74
  57.2 6.2 collective-permute-start.2
  63.4 71.1 %convolution_bitcast_fusion.3 = f32[3,7,7,7,7,7,7]{6,4,5,3,2,0,1:T(8,128)} fusion(f32[3,13,7,7,7,7]{1,2,5,3,0,4:T(8,128)S(1)} %convolution_bitcast_fusion.5, pred[7,7,13,1,1,1,1]{2,0,1,6,5,4,3:T(8,128)(4,1)S(1)} %fusion.73), kind=kOutput, calls=%fused_computation.61 | convolution fusion | flops 55059736 | bytes 1786981 | tf_op jit(solution)/shard_map/hxbcBC,aAx->habcABC/dot_general | solution.py:39
  134.6 59.5 %copy.82 = f32[3,7,7,7,7,7,7]{3,2,1,6,5,4,0:T(8,128)} copy(f32[3,7,7,7,7,7,7]{6,4,5,3,2,0,1:T(8,128)} %convolution_bitcast_fusion.3) | data formatting | bytes 2823576
  194.1 21.0 %add.230 = f32[3,343,343]{1,2,0:T(8,128)} reshape(f32[3,7,7,7,7,7,7]{3,2,1,6,5,4,0:T(8,128)} %copy.82) | data formatting | bytes 2823576 | tf_op jit(solution)/shard_map/while/body/eval_jaxpr/add | solution.py:121
  216.1 2.6 fusion.67
  224.4 2.5 copy.81
  228.8 2.5 copy.83
  231.4 134.0 %while.20 = (s32[]{:T(128)}, f32[96,288]{1,0:T(8,128)}, f32[288]{0:T(512)S(1)}, f32[96,96]{1,0:T(8,128)S(1)}, f32[3,343,343]{1,2,0:T(8,128)}, /*index=5*/f32[4,4...) while((s32[]{:T(128)}, f32[96,288]{1,0:T(8,128)}, ...), condition=%wide.wide.region_8.9_spmd.clone, body=%wide.wide.region_2.8_spmd.clone.sunk | while | flops 848489408 | bytes 107633568 | solution.py:191
  234.0 7.0 %fusion.174 = (f32[4,3,343]{2,1,0:T(4,128)S(1)}, f32[4,3,343,343]{2,3,1,0:T(8,128)}) fusion(f32[3,343,343]{1,2,0:T(8,128)} %get-tuple-element.420, pred[4,343,343]{1,2,0:T(8,128)(4,1)} %broadcast_compare_fusion.3, bf16[4,343,3,3,32]{1,4,3,2,0:T(8,128)(2,1)S(1)} %bitcast.281), kind=kOutput, calls=%fused_computation.146.clone.clone.1 | convolution fusion | flops 97413720 | bytes 8135824 | tf_op jit(solution)/shard_map/while/body/eval_jaxpr/sub | solution.py:127
  241.2 6.9 multiply_reduce_fusion.4
  248.1 4.2 fusion.176
  256.7 2.1 fusion.180
  260.1 3.6 fusion.182
  266.3 7.0 %fusion.174 = (f32[4,3,343]{2,1,0:T(4,128)S(1)}, f32[4,3,343,343]{2,3,1,0:T(8,128)}) fusion(f32[3,343,343]{1,2,0:T(8,128)} %get-tuple-element.420, pred[4,343,343]{1,2,0:T(8,128)(4,1)} %broadcast_compare_fusion.3, bf16[4,343,3,3,32]{1,4,3,2,0:T(8,128)(2,1)S(1)} %bitcast.281), kind=kOutput, calls=%fused_computation.146.clone.clone.1 | convolution fusion | flops 97413720 | bytes 8135824 | tf_op jit(solution)/shard_map/while/body/eval_jaxpr/sub | solution.py:127
  273.5 6.9 multiply_reduce_fusion.4
  280.5 4.2 fusion.176
  289.1 2.1 fusion.180
  291.2 2.7 select_add_fusion.7
  293.9 3.6 fusion.182
  300.1 7.0 %fusion.174 = (f32[4,3,343]{2,1,0:T(4,128)S(1)}, f32[4,3,343,343]{2,3,1,0:T(8,128)}) fusion(f32[3,343,343]{1,2,0:T(8,128)} %get-tuple-element.420, pred[4,343,343]{1,2,0:T(8,128)(4,1)} %broadcast_compare_fusion.3, bf16[4,343,3,3,32]{1,4,3,2,0:T(8,128)(2,1)S(1)} %bitcast.281), kind=kOutput, calls=%fused_computation.146.clone.clone.1 | convolution fusion | flops 97413720 | bytes 8135824 | tf_op jit(solution)/shard_map/while/body/eval_jaxpr/sub | solution.py:127
  307.4 6.9 multiply_reduce_fusion.4
  314.3 4.2 fusion.176
  322.9 2.1 fusion.180
  325.0 2.7 select_add_fusion.7
  327.7 3.6 fusion.182
  334.0 6.9 %fusion.174 = (f32[4,3,343]{2,1,0:T(4,128)S(1)}, f32[4,3,343,343]{2,3,1,0:T(8,128)}) fusion(f32[3,343,343]{1,2,0:T(8,128)} %get-tuple-element.420, pred[4,343,343]{1,2,0:T(8,128)(4,1)} %broadcast_compare_fusion.3, bf16[4,343,3,3,32]{1,4,3,2,0:T(8,128)(2,1)S(1)} %bitcast.281), kind=kOutput, calls=%fused_computation.146.clone.clone.1 | convolution fusion | flops 97413720 | bytes 8135824 | tf_op jit(solution)/shard_map/while/body/eval_jaxpr/sub | solution.py:127
  341.2 6.9 multiply_reduce_fusion.4
  348.1 4.2 fusion.176
  356.7 2.1 fusion.180
  358.8 2.7 select_add_fusion.7
  361.5 3.6 fusion.182
  365.4 3.4 copy.84
  371.7 20.0 %reshape.174 = f32[3,7,7,7,7,7,7]{3,2,1,6,5,4,0:T(8,128)} reshape(f32[3,343,343]{1,2,0:T(8,128)S(1)} %copy-done) | data formatting | bytes 2823576 | tf_op jit(solution)/shard_map/reshape | solution.py:47
  391.8 59.7 %copy.88 = f32[3,7,7,7,7,7,7]{1,6,4,5,3,2,0:T(8,128)} copy(f32[3,7,7,7,7,7,7]{3,2,1,6,5,4,0:T(8,128)} %reshape.174) | data formatting | bytes 2823576 | tf_op jit(solution)/shard_map/reshape | solution.py:47
  453.1 25.1 %convolution_bitcast_fusion.4 = f32[3,13,7,7,7,7]{1,5,4,3,2,0:T(8,128)} fusion(f32[3,7,7,7,7,7,7]{1,6,4,5,3,2,0:T(8,128)} %copy.88, s32[7,7]{0,1:T(8,128)S(1)} %copy-done.23), kind=kOutput, calls=%fused_computation.95 | convolution fusion | flops 55060372 | bytes 1786540 | tf_op jit(solution)/shard_map/habcABC,aAx->hxbcBC/dot_general | solution.py:48
  478.1 12.7 %copy.89 = f32[3,13,7,7,7,7]{2,3,4,5,1,0:T(8,128)} copy(f32[3,13,7,7,7,7]{1,5,4,3,2,0:T(8,128)} %convolution_bitcast_fusion.4) | data formatting | bytes 749112 | tf_op jit(solution)/shard_map/habcABC,aAx->hxbcBC/transpose | solution.py:48
  495.8 5.4 convolution_bitcast_fusion.6
  502.7 4.0 slice_reduce_fusion
  506.7 23.4 %collective-permute-done.5 = f32[28,28,3,96]{3,1,2,0:T(8,128)S(1)} collective-permute-done((f32[28,28,3,96]{3,1,2,0:T(8,128)}, f32[28,28,3,96]{3,1,2,0:T(8,128)S(1)}, u32[]{:S(2)}, u32[]{:S(2)}) %collective-permute-start.5) | collective-permute-done | bytes 903200 | tf_op jit(solution)/shard_map/ppermute | solution.py:13
  531.9 6.0 fusion.61
  540.8 8.0 %fusion.60 = bf16[28,28,7,96]{3,2,1,0:T(8,128)(2,1)} fusion(bf16[28,28,7,96]{3,2,1,0:T(8,128)(2,1)S(1)} %copy-done.2, bf16[28,28,7,96]{3,2,1,0:T(8,128)(2,1)S(1)} %copy-done.6, f32[28,28,7]{2,1,0:T(8,128)S(1)} %broadcast_multiply_fusion, f32[28,28,7]{2,1,0:T(8,128)S(1)} %broadcast_multiply_fusion.1, f32[96]{0:T(128)S(1)} %copy-done.27, ...), kind=kLoop, calls=%fused_computation.78 | loop fusion | flops 6322176 | bytes 5356672 | tf_op jit(solution)/shard_map/convert_element_type | solution.py:203
  548.8 129.1 %all-reduce.2.cloned.1.call-done = f32[43935]{0:T(1024)} async-done(((f32[43935]{0:T(1024)}), f32[43935]{0:T(1024)}) %all-reduce.2.cloned.1.call-update) | async-done | bytes 175756 | tf_op jit(solution)/shard_map/psum | solution.py:20
  (220 shorter events, 71.2 us)
Async XLA Ops:
  7.2 4.6 copy-start.26
  7.2 4.6 copy-start.28
  7.2 670.7 %all-reduce.2.cloned.1.call-start = ((), (), s32[]{:S(2)}) async-start(), calls=%async_computation | async-start | bytes 352256 | tf_op jit(solution)/shard_map/psum | solution.py:20
  9.8 4.1 copy-start.16
  9.8 5.2 copy-start.5
  13.8 4.4 copy-start.25
  15.1 15.3 %collective-permute-start = (bf16[2,3,28,7,96]{4,3,2,1,0:T(8,128)(2,1)S(1)}, bf16[2,3,28,7,96]{4,3,2,1,0:T(8,128)(2,1)S(1)}, u32[]{:S(2)}, u32[]{:S(2)}) collective-permute-start(bf16[2,3,28,7,96]{4,3,2,1,0:T(8,128)(2,1)S(1)} %pad_maximum_fusion.6), channel_id=1, source_target_pairs={{32,0},{64,32},{96,64},{0,96},{33,1},{65,33},{97,65},{1,97},{34,2}... | collective-permute-start | bytes 677384 | tf_op jit(solution)/shard_map/ppermute | solution.py:13
  18.3 30.4 %copy-start.22 = (s32[7,7]{0,1:T(8,128)}, s32[7,7]{0,1:T(8,128)S(1)}, u32[]{:S(2)}) copy-start(s32[7,7]{0,1:T(8,128)S(1)} %subtract_add_fusion) | copy-start | bytes 592
  18.5 11.0 %copy-start.12 = (bf16[1,28,28,7,96]{4,3,2,1,0:T(8,128)(2,1)S(1)}, bf16[1,28,28,7,96]{4,3,2,1,0:T(8,128)(2,1)}, u32[]{:S(2)}) copy-start(bf16[1,28,28,7,96]{4,3,2,1,0:T(8,128)(2,1)} %copy-done.11) | copy-start | bytes 3161092
  30.5 23.0 %collective-permute-start.1 = (bf16[2,28,3,7,96]{4,3,2,1,0:T(8,128)(2,1)S(1)}, bf16[2,28,3,7,96]{4,3,2,1,0:T(8,128)(2,1)S(1)}, u32[]{:S(2)}, u32[]{:S(2)}) collective-permute-start(bf16[2,28,3,7,96]{4,3,2,1,0:T(8,128)(2,1)S(1)} %pad_maximum_fusion.5), channel_id=1, source_target_pairs={{8,0},{16,8},{24,16},{0,24},{9,1},{17,9},{25,17},{1,25},{10,2},{18... | collective-permute-start | bytes 677384 | tf_op jit(solution)/shard_map/ppermute | solution.py:13
  53.5 3.7 copy-start.20
  57.2 161.6 %collective-permute-start.2 = (bf16[2,28,28,3,96]{4,0,3,2,1:T(2,128)(2,1)}, bf16[2,28,28,3,96]{4,0,3,2,1:T(2,128)(2,1)}, u32[]{:S(2)}, u32[]{:S(2)}) collective-permute-start(bf16[2,28,28,3,96]{4,0,3,2,1:T(2,128)(2,1)} %copy.74), channel_id=1, source_target_pairs={{1,0},{2,1},{3,2},{4,3},{5,4},{6,5},{7,6},{0,7},{9,8},{10,9},{11,1... | collective-permute-start | bytes 2709512 | tf_op jit(solution)/shard_map/ppermute | solution.py:13
  226.9 4.4 copy-start.17
  227.0 4.4 copy-start.21
  227.0 4.4 copy-start.24
  231.6 9.3 %copy-start.9 = (bf16[4,4,343,96]{2,3,1,0:T(8,128)(2,1)}, bf16[4,4,343,96]{2,3,1,0:T(8,128)(2,1)S(1)}, u32[]{:S(2)}) copy-start(bf16[4,4,343,96]{2,3,1,0:T(8,128)(2,1)S(1)} %get-tuple-element.413) | copy-start | bytes 3161092 | tf_op jit(solution)/shard_map/while
  231.6 9.3 %copy-start.13 = (bf16[4,4,343,96]{2,3,1,0:T(8,128)(2,1)}, bf16[4,4,343,96]{2,3,1,0:T(8,128)(2,1)S(1)}, u32[]{:S(2)}) copy-start(bf16[4,4,343,96]{2,3,1,0:T(8,128)(2,1)S(1)} %get-tuple-element.418) | copy-start | bytes 3161092 | tf_op jit(solution)/shard_map/while
  241.2 6.9 %slice-start = ((s8[6340608]{0:T(1024)(128)(4,1)}), s8[4194304]{0:T(1024)(128)(4,1)S(1)}, s32[]{:S(2)}) async-start(s8[6340608]{0:T(1024)(128)(4,1)} %bitcast.279), calls=%async_computation.1 | async-start | bytes 8388608 | tf_op jit(solution)/shard_map/while
  241.2 6.9 %slice-start.1 = ((s8[6340608]{0:T(1024)(128)(4,1)}), s8[2146304]{0:T(1024)(128)(4,1)S(1)}, s32[]{:S(2)}) async-start(s8[6340608]{0:T(1024)(128)(4,1)} %bitcast.279), calls=%async_computation.2 | async-start | bytes 4292608 | tf_op jit(solution)/shard_map/while
  260.1 3.6 copy-start.14
  260.1 3.8 copy-start.10
  263.9 9.3 %copy-start.9 = (bf16[4,4,343,96]{2,3,1,0:T(8,128)(2,1)}, bf16[4,4,343,96]{2,3,1,0:T(8,128)(2,1)S(1)}, u32[]{:S(2)}) copy-start(bf16[4,4,343,96]{2,3,1,0:T(8,128)(2,1)S(1)} %get-tuple-element.413) | copy-start | bytes 3161092 | tf_op jit(solution)/shard_map/while
  264.0 9.3 %copy-start.13 = (bf16[4,4,343,96]{2,3,1,0:T(8,128)(2,1)}, bf16[4,4,343,96]{2,3,1,0:T(8,128)(2,1)S(1)}, u32[]{:S(2)}) copy-start(bf16[4,4,343,96]{2,3,1,0:T(8,128)(2,1)S(1)} %get-tuple-element.418) | copy-start | bytes 3161092 | tf_op jit(solution)/shard_map/while
  273.5 6.9 %slice-start = ((s8[6340608]{0:T(1024)(128)(4,1)}), s8[4194304]{0:T(1024)(128)(4,1)S(1)}, s32[]{:S(2)}) async-start(s8[6340608]{0:T(1024)(128)(4,1)} %bitcast.279), calls=%async_computation.1 | async-start | bytes 8388608 | tf_op jit(solution)/shard_map/while
  273.5 6.9 %slice-start.1 = ((s8[6340608]{0:T(1024)(128)(4,1)}), s8[2146304]{0:T(1024)(128)(4,1)S(1)}, s32[]{:S(2)}) async-start(s8[6340608]{0:T(1024)(128)(4,1)} %bitcast.279), calls=%async_computation.2 | async-start | bytes 4292608 | tf_op jit(solution)/shard_map/while
  293.9 3.8 copy-start.10
  297.8 9.3 %copy-start.9 = (bf16[4,4,343,96]{2,3,1,0:T(8,128)(2,1)}, bf16[4,4,343,96]{2,3,1,0:T(8,128)(2,1)S(1)}, u32[]{:S(2)}) copy-start(bf16[4,4,343,96]{2,3,1,0:T(8,128)(2,1)S(1)} %get-tuple-element.413) | copy-start | bytes 3161092 | tf_op jit(solution)/shard_map/while
  297.8 9.3 %copy-start.13 = (bf16[4,4,343,96]{2,3,1,0:T(8,128)(2,1)}, bf16[4,4,343,96]{2,3,1,0:T(8,128)(2,1)S(1)}, u32[]{:S(2)}) copy-start(bf16[4,4,343,96]{2,3,1,0:T(8,128)(2,1)S(1)} %get-tuple-element.418) | copy-start | bytes 3161092 | tf_op jit(solution)/shard_map/while
  307.3 6.9 %slice-start = ((s8[6340608]{0:T(1024)(128)(4,1)}), s8[4194304]{0:T(1024)(128)(4,1)S(1)}, s32[]{:S(2)}) async-start(s8[6340608]{0:T(1024)(128)(4,1)} %bitcast.279), calls=%async_computation.1 | async-start | bytes 8388608 | tf_op jit(solution)/shard_map/while
  307.4 6.9 %slice-start.1 = ((s8[6340608]{0:T(1024)(128)(4,1)}), s8[2146304]{0:T(1024)(128)(4,1)S(1)}, s32[]{:S(2)}) async-start(s8[6340608]{0:T(1024)(128)(4,1)} %bitcast.279), calls=%async_computation.2 | async-start | bytes 4292608 | tf_op jit(solution)/shard_map/while
  327.7 3.6 copy-start.14
  327.7 3.8 copy-start.10
  331.6 9.3 %copy-start.9 = (bf16[4,4,343,96]{2,3,1,0:T(8,128)(2,1)}, bf16[4,4,343,96]{2,3,1,0:T(8,128)(2,1)S(1)}, u32[]{:S(2)}) copy-start(bf16[4,4,343,96]{2,3,1,0:T(8,128)(2,1)S(1)} %get-tuple-element.413) | copy-start | bytes 3161092 | tf_op jit(solution)/shard_map/while
  331.6 9.3 %copy-start.13 = (bf16[4,4,343,96]{2,3,1,0:T(8,128)(2,1)}, bf16[4,4,343,96]{2,3,1,0:T(8,128)(2,1)S(1)}, u32[]{:S(2)}) copy-start(bf16[4,4,343,96]{2,3,1,0:T(8,128)(2,1)S(1)} %get-tuple-element.418) | copy-start | bytes 3161092 | tf_op jit(solution)/shard_map/while
  341.1 6.9 %slice-start = ((s8[6340608]{0:T(1024)(128)(4,1)}), s8[4194304]{0:T(1024)(128)(4,1)S(1)}, s32[]{:S(2)}) async-start(s8[6340608]{0:T(1024)(128)(4,1)} %bitcast.279), calls=%async_computation.1 | async-start | bytes 8388608 | tf_op jit(solution)/shard_map/while
  341.2 6.9 %slice-start.1 = ((s8[6340608]{0:T(1024)(128)(4,1)}), s8[2146304]{0:T(1024)(128)(4,1)S(1)}, s32[]{:S(2)}) async-start(s8[6340608]{0:T(1024)(128)(4,1)} %bitcast.279), calls=%async_computation.2 | async-start | bytes 4292608 | tf_op jit(solution)/shard_map/while
  361.5 3.8 copy-start.10
  370.0 81.5 %collective-permute-start.3 = (f32[3,28,7,96]{3,2,1,0:T(8,128)}, f32[3,28,7,96]{3,2,1,0:T(8,128)S(1)}, u32[]{:S(2)}, u32[]{:S(2)}) collective-permute-start(f32[3,28,7,96]{3,2,1,0:T(8,128)} %slice.103), channel_id=1, source_target_pairs={{96,0},{0,32},{32,64},{64,96},{97,1},{1,33},{33,65},{65,97},{98,2}... | collective-permute-start | bytes 677384 | tf_op jit(solution)/shard_map/ppermute | solution.py:13
  391.8 59.7 %copy-start.4 = (f32[25,28,7,96]{3,2,1,0:T(8,128)S(1)}, f32[25,28,7,96]{3,2,1,0:T(8,128)}, u32[]{:S(2)}) copy-start(f32[25,28,7,96]{3,2,1,0:T(8,128)} %slice.104) | copy-start | bytes 5644804
  452.2 38.6 %collective-permute-start.4 = (f32[28,3,7,96]{3,2,1,0:T(8,128)}, f32[28,3,7,96]{3,2,1,0:T(8,128)}, u32[]{:S(2)}, u32[]{:S(2)}) collective-permute-start(f32[28,3,7,96]{3,2,1,0:T(8,128)} %pad_maximum_fusion.4), channel_id=1, source_target_pairs={{24,0},{0,8},{8,16},{16,24},{25,1},{1,9},{9,17},{17,25},{26,2},{2,... | collective-permute-start | bytes 677384 | tf_op jit(solution)/shard_map/ppermute | solution.py:13
  490.8 5.0 copy-start.3
  492.4 8.8 %copy-start.15 = (f32[28,28,7,96]{3,2,1,0:T(8,128)}, f32[28,28,7,96]{3,2,1,0:T(8,128)S(1)}, u32[]{:S(2)}) copy-start(f32[28,28,7,96]{3,2,1,0:T(8,128)S(1)} %fusion.63) | copy-start | bytes 6322180
  494.1 8.4 %copy-start.19 = (f32[96,288]{1,0:T(8,128)S(1)}, f32[96,288]{1,0:T(8,128)}, u32[]{:S(2)}) copy-start(f32[96,288]{1,0:T(8,128)} %get-tuple-element.79) | copy-start | bytes 331780
  494.1 36.1 %collective-permute-start.5 = (f32[28,28,3,96]{3,1,2,0:T(8,128)}, f32[28,28,3,96]{3,1,2,0:T(8,128)S(1)}, u32[]{:S(2)}, u32[]{:S(2)}) collective-permute-start(f32[28,28,3,96]{3,1,2,0:T(8,128)} %copy.86), channel_id=1, source_target_pairs={{7,0},{0,1},{1,2},{2,3},{3,4},{4,5},{5,6},{6,7},{15,8},{8,9},{9,10... | collective-permute-start | bytes 2709512 | tf_op jit(solution)/shard_map/ppermute | solution.py:13
  502.7 28.8 %copy-start.2 = (bf16[28,28,7,96]{3,2,1,0:T(8,128)(2,1)S(1)}, bf16[28,28,7,96]{3,2,1,0:T(8,128)(2,1)}, u32[]{:S(2)}) copy-start(bf16[28,28,7,96]{3,2,1,0:T(8,128)(2,1)} %param.10) | copy-start | bytes 3161092
  502.7 28.8 %copy-start.27 = (f32[96]{0:T(128)S(1)}, f32[96]{0:T(128)}, u32[]{:S(2)}) copy-start(f32[96]{0:T(128)} %param.12) | copy-start | bytes 1156
  531.5 6.4 copy-start.8
  531.9 8.9 %copy-start.6 = (bf16[28,28,7,96]{3,2,1,0:T(8,128)(2,1)S(1)}, bf16[28,28,7,96]{3,2,1,0:T(8,128)(2,1)}, u32[]{:S(2)}) copy-start(bf16[28,28,7,96]{3,2,1,0:T(8,128)(2,1)} %param.11) | copy-start | bytes 3161092
  (8 other events, 19.8 us)
Sparse Core Ops, SparseCore 0:
  538.8 139.1 all-reduce.1
where the time goes:
time: 702 us; the launch traced here: 692 us
  matrix products  211 us (30%)
  local copies, waits for them, and re-layouts  207 us (29%)
  waiting for transfers between devices  156 us (22%)
  other arithmetic  74.5 us (11%)
  starting transfers between devices  28.6 us (4%)
  between operations  14.8 us (2%)
    psum x1, waiting for transfers between devices, in_one(): so_far = lax.psum(jnp.concatenate([a.ravel() for a in arrays]), axis)  129 us
    reshape x2, local copies, waits for them, and re-layouts, fold_table(): grid = pairs.reshape(heads, span, span, span, span, span, span)  79.7 us
    dot_general x1, matrix products, expand_table(): section = jnp.einsum('hxbcBC,aAx->habcABC', section, ones, precision=exact)  71.1 us
    unnamed x53, local copies, waits for them, and re-layouts  67.9 us
    ppermute x6, starting transfers between devices, shifted(): return lax.ppermute(block, axis, route)  28.6 us
    sub x4, matrix products, window_pass(): expo = jnp.exp(scores - top)  27.8 us
    dot_general x4, matrix products, window_pass(): jnp.einsum('ghid,ghjd->ghij', grad_heads, values, preferred_element_type=...  27.7 us
    ppermute x6, waiting for transfers between devices, shifted(): return lax.ppermute(block, axis, route)  27.4 us
  transfers between devices with their start and end apart: 7, of which 3 were waited for; matrix products, arithmetic and copies ran while one was open for 45% of the time, Pallas kernels for 0%

commit v1 on v0

v1 whole, which is shorter than its diff:
```python
import functools

import jax
import jax.numpy as jnp
import numpy as np
from jax import lax
from jax.experimental import pallas as pl
from jax.experimental.pallas import tpu as pltpu
from jax.sharding import PartitionSpec as P

WIN = 7
SHIFT = 3
TOK = WIN**3
ROWS = 352
LANES = 384
FEATS = 96
HEADS = 3
HDIM = 32
PLANE = 49
WIDTH = 13
TABLE = WIDTH**3
SPREAD = 2304
SQUEEZED = 640
FAR = -(2.0**100)
NEVER = -1e30
LOG2E = 1.4426950408889634
SCALE = HDIM**-0.5
F32 = jnp.float32
BF16 = jnp.bfloat16


def nn(a, b):
    return lax.dot_general(a, b, (((1,), (0,)), ((), ())), preferred_element_type=F32)


def nt(a, b):
    return lax.dot_general(a, b, (((1,), (1,)), ((), ())), preferred_element_type=F32)


def squeeze_ones():
    lane = np.arange(SQUEEZED)
    place = lane // 49 * 169 + lane % 49 // 7 * 13 + lane % 7
    return (np.arange(SPREAD)[:, None] == np.where(lane < 637, place, -1)[None, :]).astype(np.float32)


def token_features():
    token = np.arange(ROWS)
    late = np.stack([token // 49 >= 4, token % 49 // 7 >= 4, token % 7 >= 4]).astype(np.float32)
    return late


def key_features():
    late = token_features()
    out = np.zeros((ROWS, 256), np.float32)
    for d in range(3):
        out[:, 96 + 2 * d] = late[d]
        out[:, 97 + 2 * d] = 1 - late[d]
    return out


def query_features():
    token = np.arange(LANES)
    late = np.stack([token // 49 >= 4, token % 49 // 7 >= 4, token % 7 >= 4]).astype(np.float32)
    out = np.zeros((3, 16, LANES), np.float32)
    for d in range(3):
        out[d, 2 * d] = FAR * (1 - late[d])
        out[d, 2 * d + 1] = FAR * late[d]
    return out


def pieces(x, count):
    out = []
    for _ in range(count):
        piece = x.astype(BF16)
        out.append(piece)
        x = x - piece.astype(F32)
    return out


def expand_table(table_ref, ones_ref, bias_ref, wide_ref, flat_ref):
    for h in range(HEADS):
        row = jnp.broadcast_to(table_ref[h : h + 1, :] * LOG2E, (8, SPREAD))
        row = pltpu.roll(row, 0, 1, stride=1, stride_axis=0)
        for jy in range(WIN):
            moved = pltpu.roll(row, SPREAD - 13 * (6 - jy) - 6, 1)
            for n, piece in enumerate(pieces(moved, 3)):
                wide_ref[n, h * 56 + jy * 8 : h * 56 + jy * 8 + 8, :] = piece.astype(F32)
    total = None
    for n in range(3):
        part = nn(wide_ref[n].astype(BF16), ones_ref[...])
        total = part if total is None else total + part
    flat_ref[...] = total
    lane = lax.broadcasted_iota(jnp.int32, (8, LANES), 1)
    for h in range(HEADS):
        for jx in range(WIN):
            turned = pltpu.roll(flat_ref[h * 56 : h * 56 + 56, :], (SQUEEZED - 49 * (6 - jx)) % SQUEEZED, 1)
            for jy in range(WIN):
                bias_ref[h, pl.ds(jx * 49 + jy * 7, 8), :] = jnp.where(
                    lane < TOK, turned[jy * 8 : jy * 8 + 8, :LANES], 0.0
                )
        bias_ref[h, TOK : TOK + 9, :] = jnp.full((9, LANES), NEVER, F32)


def fold_table(sums_ref, ones_ref, wide_ref, flat_ref, out_ref):
    flat_ref[...] = jnp.zeros((HEADS * 56, SQUEEZED), F32)
    sub = lax.broadcasted_iota(jnp.int32, (8, SQUEEZED), 0)
    for h in range(HEADS):
        for jy in range(WIN):
            total = jnp.zeros((8, SQUEEZED), F32)
            for jx in range(WIN):
                block = sums_ref[h, pl.ds(jx * 49 + jy * 7, 8), :]
                block = jnp.concatenate([block, jnp.zeros((8, SQUEEZED - LANES), F32)], 1)
                total = total + pltpu.roll(block, 49 * (6 - jx), 1)
            flat_ref[h * 56 + jy * 8 : h * 56 + jy * 8 + 8, :] = jnp.where(sub < WIN, total, 0.0)
    spread = None
    for piece in pieces(flat_ref[...], 3):
        part = nt(piece, ones_ref[...])
        spread = part if spread is None else spread + part
    wide_ref[0] = spread
    for h in range(HEADS):
        total = jnp.zeros((8, SPREAD), F32)
        for jy in range(WIN):
            block = wide_ref[0, h * 56 + jy * 8 : h * 56 + jy * 8 + 8, :]
            total = total + pltpu.roll(block, 13 * (6 - jy), 1)
        line = jnp.zeros((1, SPREAD), F32)
        for jz in range(WIN):
            line = line + pltpu.roll(total, 6 - jz, 1)[jz : jz + 1]
        out_ref[h : h + 1, :] = line


def window_kernel(
    cells_x,
    cells_y,
    x_ref,
    dy_ref,
    gain_ref,
    shift_ref,
    table_ref,
    ones_ref,
    w_all_ref,
    w_kv_ref,
    b_col_ref,
    b_kv_ref,
    q_feat_ref,
    w_proj_ref,
    w_qkv_ref,
    dx_ref,
    wq_ref,
    wkv_ref,
    proj_ref,
    rel_ref,
    rows_ref,
    bq_ref,
    bias_ref,
    acc_ref,
    e_ref,
    ds_ref,
    q_ref,
    do_ref,
    ln_ref,
    gq_ref,
    wide_ref,
    flat_ref,
):
    step = pl.program_id(0)

    @pl.when(step == 0)
    def _():
        expand_table(table_ref, ones_ref, bias_ref, wide_ref, flat_ref)
        acc_ref[...] = jnp.zeros_like(acc_ref)
        e_ref[...] = jnp.zeros_like(e_ref)
        ds_ref[...] = jnp.zeros_like(ds_ref)
        q_ref[...] = jnp.zeros_like(q_ref)
        do_ref[...] = jnp.zeros_like(do_ref)
        wq_ref[...] = jnp.zeros_like(wq_ref)
        wkv_ref[...] = jnp.zeros_like(wkv_ref)
        proj_ref[...] = jnp.zeros_like(proj_ref)
        rows_ref[...] = jnp.zeros_like(rows_ref)
        bq_ref[...] = jnp.zeros_like(bq_ref)
        gq_ref[...] = jnp.zeros_like(gq_ref)
        ln_ref[...] = jnp.zeros_like(ln_ref)

    wins_y = cells_y // WIN
    wins_x = cells_x // WIN
    last_x = (lax.axis_index("gx") == lax.axis_size("gx") - 1) & (step // wins_y == wins_x - 1)
    last_y = (lax.axis_index("gy") == lax.axis_size("gy") - 1) & (step % wins_y == wins_y - 1)
    last_z = lax.axis_index("gz") == lax.axis_size("gz") - 1

    x = x_ref[0].astype(F32)
    mean = jnp.mean(x, -1, keepdims=True)
    centered = x - mean
    rstd = lax.rsqrt(jnp.mean(centered * centered, -1, keepdims=True) + 1e-05)
    xhat = centered * rstd
    ln_ref[0:ROWS, :] = (xhat * gain_ref[...] + shift_ref[...]).astype(BF16)

    across = nt(w_all_ref[...], ln_ref[...])
    q_t = ((across[0:96] + b_col_ref[0:96]) * (SCALE * LOG2E)).astype(BF16)
    k_t = (across[96:192] + b_col_ref[96:192]).astype(BF16)
    v_t = (across[192:288] + b_col_ref[192:288]).astype(BF16)
    ln_t = across[288:384].astype(BF16)
    marks = (
        q_feat_ref[0] * last_x.astype(F32)
        + q_feat_ref[1] * last_y.astype(F32)
        + q_feat_ref[2] * last_z.astype(F32)
    ).astype(BF16)
    for h in range(HEADS):
        q_ref[h * HDIM : (h + 1) * HDIM, h * LANES : (h + 1) * LANES] = q_t[h * HDIM : (h + 1) * HDIM]
        q_ref[96:112, h * LANES : (h + 1) * LANES] = marks
    kv = nn(ln_ref[0:ROWS, :], w_kv_ref[...]) + b_kv_ref[...]
    k = kv[:, 0:128].astype(BF16)
    v = kv[:, 128:256].astype(BF16)
    dy = dy_ref[0]
    do_t = nt(w_proj_ref[...], dy)

    att = []
    for h in range(HEADS):
        inverse = []
        for c in range(3):
            at = pl.ds(h * LANES + c * 128, 128)
            s = nn(k, q_ref[:, at]) + bias_ref[h, :, pl.ds(c * 128, 128)]
            e = jnp.exp2(s - jnp.max(s, 0, keepdims=True))
            inv = 1.0 / jnp.sum(e, 0, keepdims=True)
            inverse.append(inv)
            e_ref[0:ROWS, at] = e.astype(BF16)
            do_ref[h * HDIM : (h + 1) * HDIM, at] = (
                do_t[h * HDIM : (h + 1) * HDIM, c * 128 : c * 128 + 128] * inv
            ).astype(BF16)
            dp = nn(v, do_ref[:, at])
            ds = e * (dp - jnp.sum(e * dp, 0, keepdims=True) * inv)
            acc_ref[h, :, pl.ds(c * 128, 128)] += ds
            ds_ref[0:ROWS, at] = ds.astype(BF16)
        at = pl.ds(h * LANES, LANES)
        inverse = jnp.concatenate(inverse, 1)
        o_t = nn(v_t[h * HDIM : (h + 1) * HDIM], e_ref[:, at]) * inverse
        att.append(o_t.astype(BF16))
        gq_ref[h * HDIM : (h + 1) * HDIM, :] = nn(k_t[h * HDIM : (h + 1) * HDIM], ds_ref[:, at]) * SCALE
    att = jnp.concatenate(att, 0)
    proj_ref[...] += nn(att, dy)
    grad_v = nt(e_ref[0:ROWS, :], do_ref[...])
    grad_k = nt(ds_ref[0:ROWS, :], q_ref[0:96, :]) * (1.0 / LOG2E)
    gq = gq_ref[...]
    bq_ref[...] += gq[0:96, 0:128] + gq[0:96, 128:256] + gq[0:96, 256:384]
    wq_ref[...] += nn(gq[0:96].astype(BF16), ln_ref[...])
    grad_q = gq.T[0:ROWS, 0:96].astype(BF16)
    grad_v = grad_v[:, 0:96]
    k_b = grad_k.astype(BF16)
    v_b = grad_v.astype(BF16)
    wkv_ref[:, 0:96] += nn(ln_t[:, 0:ROWS], k_b)
    wkv_ref[:, 128:224] += nn(ln_t[:, 0:ROWS], v_b)
    grad_in = (
        nt(grad_q, w_qkv_ref[:, 0:96])
        + nt(k_b, w_qkv_ref[:, 128:224])
        + nt(v_b, w_qkv_ref[:, 256:352])
    )
    rows_ref[0] += jnp.sum(grad_k.reshape(ROWS // 8, 8, 96), 0)
    rows_ref[1] += jnp.sum(grad_v.reshape(ROWS // 8, 8, 96), 0)
    rows_ref[2] += jnp.sum((xhat * grad_in).reshape(ROWS // 8, 8, 96), 0)
    rows_ref[3] += jnp.sum(grad_in.reshape(ROWS // 8, 8, 96), 0)
    dhat = grad_in * gain_ref[...]
    first = jnp.mean(dhat, -1, keepdims=True)
    second = jnp.mean(dhat * xhat, -1, keepdims=True)
    dx_ref[0] = (dy[0:ROWS].astype(F32) + rstd * (dhat - first - xhat * second)).astype(BF16)

    @pl.when(step == pl.num_programs(0) - 1)
    def _():
        fold_table(acc_ref, ones_ref, wide_ref, flat_ref, rel_ref)


def window_call(win_x, win_dy, gain, shift, table, w_qkv, b_qkv, w_proj, cells_x, cells_y):
    count = win_x.shape[0]
    ones = jnp.asarray(squeeze_ones(), BF16)
    w_t = w_qkv.T
    w_all = jnp.concatenate([w_t, jnp.eye(96, dtype=BF16)], 0)
    gap = jnp.zeros((96, 32), BF16)
    w_k, w_v = w_qkv[:, 96:192], w_qkv[:, 192:288]
    w_kv = jnp.concatenate([w_k, gap, w_v, gap], 1)
    w_back = jnp.concatenate([w_qkv[:, 0:96], gap, w_k, gap, w_v, gap], 1)
    gap_b = jnp.zeros((32,), F32)
    b_row = jnp.concatenate([b_qkv[96:192], gap_b, b_qkv[192:288], gap_b])
    b_kv = jnp.asarray(key_features()) + b_row[None, :]
    b_col = b_qkv[:, None]
    table = jnp.pad(table, ((0, 5), (0, SPREAD - TABLE)))
    whole = lambda a: pl.BlockSpec(a.shape, lambda i: (0,) * a.ndim)
    tile = lambda rows: pl.BlockSpec((1, rows, FEATS), lambda i: (i, 0, 0))
    consts = (gain[None, :], shift[None, :], table, ones, w_all, w_kv, b_col, b_kv)
    consts += (jnp.asarray(query_features()), w_proj, w_back)
    outs = (
        jax.ShapeDtypeStruct((count, ROWS, FEATS), BF16),
        jax.ShapeDtypeStruct((96, 96), F32),
        jax.ShapeDtypeStruct((96, 256), F32),
        jax.ShapeDtypeStruct((96, 96), F32),
        jax.ShapeDtypeStruct((8, SPREAD), F32),
        jax.ShapeDtypeStruct((4, 8, 96), F32),
        jax.ShapeDtypeStruct((96, 128), F32),
    )
    return pl.pallas_call(
        functools.partial(window_kernel, cells_x, cells_y),
        grid=(count,),
        in_specs=[tile(LANES)] * 0 + [tile(ROWS), tile(LANES)] + [whole(a) for a in consts],
        out_specs=[tile(ROWS)] + [whole(a) for a in outs[1:]],
        out_shape=outs,
        scratch_shapes=[
            pltpu.VMEM((HEADS, ROWS, LANES), F32),
            pltpu.VMEM((HEADS, ROWS, LANES), F32),
            pltpu.VMEM((LANES, HEADS * LANES), BF16),
            pltpu.VMEM((LANES, HEADS * LANES), BF16),
            pltpu.VMEM((128, HEADS * LANES), BF16),
            pltpu.VMEM((128, HEADS * LANES), BF16),
            pltpu.VMEM((LANES, FEATS), BF16),
            pltpu.VMEM((128, LANES), F32),
            pltpu.VMEM((3, HEADS * 56, SPREAD), F32),
            pltpu.VMEM((HEADS * 56, SQUEEZED), F32),
        ],
        compiler_params=pltpu.CompilerParams(vmem_limit_bytes=56 << 20),
        cost_estimate=pl.CostEstimate(flops=5 * 10**9, bytes_accessed=6 * 10**6, transcendentals=6 * 10**6),
    )(win_x, win_dy, *consts)


def shifted(block, axis, distance):
    devices = range(lax.axis_size(axis))
    route = [((i - distance) % len(devices), i) for i in devices]
    return lax.ppermute(block, axis, route)


def in_one(arrays, axis):
    ends = [0]
    for a in arrays:
        ends.append(ends[-1] + a.size)
    so_far = lax.psum(jnp.concatenate([a.ravel() for a in arrays]), axis)
    return tuple(so_far[b:e].reshape(a.shape) for a, b, e in zip(arrays, ends, ends[1:]))


def to_windows(array, rows):
    first, second, third, rest = array.shape
    shaped = array.reshape(first // WIN, WIN, second // WIN, WIN, third // WIN, WIN, rest)
    flat = shaped.transpose(0, 2, 4, 1, 3, 5, 6).reshape(-1, TOK, rest)
    return jnp.pad(flat, ((0, 0), (0, rows - TOK), (0, 0)))


def from_windows(array, first, second, third):
    feats = array.shape[-1]
    shaped = array.reshape(first // WIN, second // WIN, third // WIN, WIN, WIN, WIN, feats)
    return shaped.transpose(0, 3, 1, 4, 2, 5, 6).reshape(first, second, third, feats)


def forward(pair, dim, axis):
    head = lax.slice_in_dim(pair, 0, SHIFT, axis=dim)
    rest = lax.slice_in_dim(pair, SHIFT, pair.shape[dim], axis=dim)
    return jnp.concatenate([rest, shifted(head, axis, -1)], dim)


def backward(field, dim, axis):
    edge = field.shape[dim] - SHIFT
    tail = lax.slice_in_dim(field, edge, field.shape[dim], axis=dim)
    rest = lax.slice_in_dim(field, 0, edge, axis=dim)
    return jnp.concatenate([shifted(tail, axis, 1), rest], dim)


def shards(inputs, d_out, gain, shift, w_qkv, b_qkv, w_proj, rel_bias):
    cells_x, cells_y, cells_z, _ = inputs.shape
    pair = jnp.stack([inputs, d_out])
    axes = ("gx", "gy", "gz")
    for d, axis in enumerate(axes):
        pair = forward(pair, d + 1, axis)
    win_x = to_windows(pair[0], ROWS)
    win_dy = to_windows(pair[1], LANES)
    dx, wq, wkv, proj, rel, rows, bq = window_call(
        win_x, win_dy, gain, shift, rel_bias, w_qkv, b_qkv, w_proj, cells_x, cells_y
    )
    field = from_windows(dx[:, :TOK], cells_x, cells_y, cells_z)
    for d, axis in enumerate(axes):
        field = backward(field, d, axis)
    sums = jnp.sum(rows, 1)
    bq = jnp.sum(bq, 1)
    weight = jnp.concatenate([wq.T, wkv[:, 0:96], wkv[:, 128:224]], 1)
    bias = jnp.concatenate([bq, sums[0], sums[1]])
    rel = rel[:HEADS, :TABLE]
    count = inputs.size // FEATS * lax.axis_size("gx") * lax.axis_size("gy") * lax.axis_size("gz")
    factor = float(count) ** -0.5
    totals = in_one((weight, bias, proj, rel, sums[2], sums[3]), axes)
    return (field,) + tuple(t * factor for t in totals)


def solution(mesh):
    placed = (P("gx", "gy", "gz", None), P("gx", "gy", "gz", None), P(), P(), P(), P(), P(), P())
    return jax.shard_map(
        shards,
        mesh=mesh,
        in_specs=placed,
        out_specs=(P("gx", "gy", "gz", None), P(), P(), P(), P(), P(), P()),
        check_vma=False,
    )
```

time: 702 us -> 326 us (0.46); the launches traced: 692 us -> 325 us
  matrix products: 211 us -> 0 us
  local copies, waits for them, and re-layouts: 207 us -> 23.6 us
  Pallas kernels: 0 us -> 66.7 us
  other arithmetic: 74.5 us -> 20.1 us
  waiting for transfers between devices: 156 us -> 187 us
  starting transfers between devices: 28.6 us -> 13.1 us
    dot_general x46 -> x0, matrix products: 183 us -> none  [the longest x1 71.1 us: expand_table(): section = jnp.einsum('hxbcBC,aAx->habcABC', section, ones, precision=exact)]
    reshape x3 -> x2, local copies, waits for them, and re-layouts: 79.9 us -> 0.73 us  [to_windows(): flat = shaped.transpose(0, 2, 4, 1, 3, 5, 6).reshape(-1, TOK, rest)]
    pallas_call x0 -> x1, Pallas kernels: none -> 66.7 us  [window_call(): pl.pallas_call(functools.partial(window_kernel, cells_x, cells_y), grid=(...]
    unnamed x53 -> x27, local copies, waits for them, and re-layouts: 67.9 us -> 1.68 us
    reduce_sum x14 -> x2, other arithmetic: 32.2 us -> 1.64 us  [the longest x1 0.9 us: shards(): bq = jnp.sum(bq, 1)]
    sub x4 -> x0, matrix products: 27.8 us -> none  [window_pass(): expo = jnp.exp(scores - top)]
    add x1 -> x0, local copies, waits for them, and re-layouts: 21 us -> none  [window_pass(): jnp.einsum('ghid,ghjd->ghij', query, keys, preferred_element_type=f32)]
    ppermute x6, waiting for transfers between devices: 27.4 us -> 45 us  [shifted(): return lax.ppermute(block, axis, route)]
  transfers between devices with their start and end apart: 7 -> 7, of which waited for: 3 -> 5; matrix products, arithmetic and copies ran while one was open for 45% -> 7% of each run, Pallas kernels for 0% -> 0%
where the time goes in v1:
time: 326 us; the launch traced here: 325 us
  waiting for transfers between devices  187 us (57%)
  Pallas kernels  66.7 us (20%)
  local copies, waits for them, and re-layouts  23.6 us (7%)
  other arithmetic  20.1 us (6%)
  between operations  14.4 us (4%)
  starting transfers between devices  13.1 us (4%)
    psum x1, waiting for transfers between devices, in_one(): so_far = lax.psum(jnp.concatenate([a.ravel() for a in arrays]), axis)  142 us
    pallas_call x1, Pallas kernels, window_call(): pl.pallas_call(functools.partial(window_kernel, cells_x, cells_y), grid=(...  66.7 us
    ppermute x6, waiting for transfers between devices, shifted(): return lax.ppermute(block, axis, route)  45 us
    ppermute x6, starting transfers between devices, shifted(): return lax.ppermute(block, axis, route)  13 us
  transfers between devices with their start and end apart: 7, of which 5 were waited for; matrix products, arithmetic and copies ran while one was open for 7% of the time, Pallas kernels for 0%

profile of v1, /device:TPU:0, one launch (start us, length us, event | category | flops | bytes accessed | tf_op | source)
XLA Modules:
  0.0 325.3 jit_solution(17619942711259282654)
XLA Ops:
  7.2 1.2 pad_maximum_fusion.5
  8.5 3.2 collective-permute-start
  11.7 0.8 fusion.1
  12.5 0.7 fusion.7
  13.2 5.8 %collective-permute-done = bf16[2,3,28,7,96]{4,3,2,1,0:T(8,128)(2,1)S(1)} collective-permute-done((bf16[2,3,28,7,96]{4,3,2,1,0:T(8,128)(2,1)S(1)}, bf16[2,3,28,7,96]{4,3,2,1,0:T(8,128)(2,1)S(1)}, u32[]{:S(2)}, u32[]{:S(2)}) %collective-permute-start) | collective-permute-done | bytes 225824 | tf_op jit(solution)/shard_map/ppermute | solution.py:322
  19.0 0.8 pad_maximum_fusion.4
  19.9 0.6 fusion.8
  20.5 1.6 copy.57
  22.1 1.4 broadcast_in_dim.21.b_col_ref
  23.5 1.4 pad.14.table_ref
  24.9 0.6 broadcast_in_dim.18
  25.5 1.6 concatenate.42.w_qkv_ref
  27.1 0.7 fusion
  27.9 0.8 pad_maximum_fusion.2
  28.8 1.9 copy.51
  30.7 6.7 %collective-permute-start.2 = (bf16[2,28,28,3,96]{4,0,3,2,1:T(2,128)(2,1)S(1)}, bf16[2,28,28,3,96]{4,0,3,2,1:T(2,128)(2,1)S(1)}, u32[]{:S(2)}, u32[]{:S(2)}) collective-permute-start(bf16[2,28,28,3,96]{4,0,3,2,1:T(2,128)(2,1)S(1)} %copy.51), channel_id=1, source_target_pairs={{1,0},{2,1},{3,2},{4,3},{5,4},{6,5},{7,6},{0,7},{9,8},{10,9},{11,1... | collective-permute-start | bytes 2709512 | tf_op jit(solution)/shard_map/ppermute | solution.py:322
  37.5 0.7 pad_maximum_fusion.9.w_kv_ref
  38.2 0.7 pad_maximum_fusion.8.w_all_ref
  38.9 0.8 broadcast_add_fusion.b_kv_ref
  39.6 1.7 fusion.3
  41.3 22.5 %collective-permute-done.2 = bf16[2,28,28,3,96]{4,0,3,2,1:T(2,128)(2,1)S(1)} collective-permute-done((bf16[2,28,28,3,96]{4,0,3,2,1:T(2,128)(2,1)S(1)}, bf16[2,28,28,3,96]{4,0,3,2,1:T(2,128)(2,1)S(1)}, u32[]{:S(2)}, u32[]{:S(2)}) %collective-permute-start.2) | collective-permute-done | bytes 903200 | tf_op jit(solution)/shard_map/ppermute | solution.py:322
  64.2 2.1 pad_maximum_fusion.1
  66.3 0.6 copy.55
  67.2 1.5 pad.13.dy_ref
  68.8 0.6 copy.53
  69.7 1.4 pad.12.x_ref
  71.1 66.7 %shard_map.162 = (bf16[16,352,96]{2,1,0:T(8,128)(2,1)}, f32[96,96]{1,0:T(8,128)}, f32[96,256]{1,0:T(8,128)}, f32[96,96]{1,0:T(8,128)}, f32[8,2304]{1,0:T(8,128)}...) custom-call(bf16[16,352,96]{2,1,0:T(8,128)(2,1)} %pad.12.x_ref, bf16[16,384,96]{2,1,0:T(8,128)(2,1)} %pad.13.dy_ref, ...), custom_call_target="tpu_custom_call" | custom-call | flops 5000000000 | bytes 6000000 | tf_op jit(solution)/shard_map/pallas_call | solution.py:296
  137.8 0.9 fusion.6
  138.8 0.9 copy.63
  139.9 0.7 reduce_sum.19
  140.7 0.9 slice.123
  141.6 0.9 reshape.50
  142.5 0.9 reduce_sum.18
  143.5 0.8 concatenate.47
  145.1 1.1 collective-permute-start.3
  146.2 142.5 %all-reduce.5.cloned.1.call-done = f32[43935]{0:T(1024)} async-done(((f32[43935]{0:T(1024)}), f32[43935]{0:T(1024)}) %all-reduce.5.cloned.1.call-update) | async-done | bytes 175756 | tf_op jit(solution)/shard_map/psum | solution.py:329
  288.7 0.9 slice_multiply_fusion
  290.2 0.9 slice_multiply_fusion.1
  291.1 3.5 %collective-permute-done.4 = bf16[28,3,7,96]{3,2,1,0:T(8,128)(2,1)S(1)} collective-permute-done((bf16[28,3,7,96]{3,2,1,0:T(8,128)(2,1)S(1)}, bf16[28,3,7,96]{3,2,1,0:T(8,128)(2,1)S(1)}, u32[]{:S(2)}, u32[]{:S(2)}) %collective-permute-start.4) | collective-permute-done | bytes 112928 | tf_op jit(solution)/shard_map/ppermute | solution.py:322
  295.6 1.5 collective-permute-start.5
  297.0 0.8 slice_multiply_fusion.2
  297.9 0.8 mul.41
  298.6 0.7 mul.46
  299.3 0.7 mul.49
  300.0 1.3 slice_multiply_fusion.4
  301.4 1.3 slice_multiply_fusion.3
  302.6 13.2 %collective-permute-done.5 = bf16[28,28,3,96]{3,1,2,0:T(8,128)(2,1)S(1)} collective-permute-done((bf16[28,28,3,96]{3,1,2,0:T(8,128)(2,1)S(1)}, bf16[28,28,3,96]{3,1,2,0:T(8,128)(2,1)S(1)}, u32[]{:S(2)}, u32[]{:S(2)}) %collective-permute-start.5) | collective-permute-done | bytes 451616 | tf_op jit(solution)/shard_map/ppermute | solution.py:322
  316.3 2.2 pad_maximum_fusion.3
  (54 shorter events, 4.6 us)
Async XLA Ops:
  7.2 281.5 %all-reduce.5.cloned.1.call-start = ((), (), s32[]{:S(2)}) async-start(), calls=%async_computation | async-start | bytes 352256 | tf_op jit(solution)/shard_map/psum | solution.py:329
  7.2 4.5 %copy-start = (bf16[28,28,7,96]{3,2,1,0:T(8,128)(2,1)S(1)}, bf16[28,28,7,96]{3,2,1,0:T(8,128)(2,1)}, u32[]{:S(2)}) copy-start(bf16[28,28,7,96]{3,2,1,0:T(8,128)(2,1)} %param.12) | copy-start | bytes 3161092
  7.2 4.4 %copy-start.1 = (bf16[28,28,7,96]{3,2,1,0:T(8,128)(2,1)S(1)}, bf16[28,28,7,96]{3,2,1,0:T(8,128)(2,1)}, u32[]{:S(2)}) copy-start(bf16[28,28,7,96]{3,2,1,0:T(8,128)(2,1)} %param.11) | copy-start | bytes 3161092
  8.5 4.0 %copy-start.7 = (bf16[96,288]{1,0:T(8,128)(2,1)S(1)}, bf16[96,288]{1,0:T(8,128)(2,1)}, u32[]{:S(2)}) copy-start(bf16[96,288]{1,0:T(8,128)(2,1)} %param.15) | copy-start | bytes 165892
  8.5 10.5 %collective-permute-start = (bf16[2,3,28,7,96]{4,3,2,1,0:T(8,128)(2,1)S(1)}, bf16[2,3,28,7,96]{4,3,2,1,0:T(8,128)(2,1)S(1)}, u32[]{:S(2)}, u32[]{:S(2)}) collective-permute-start(bf16[2,3,28,7,96]{4,3,2,1,0:T(8,128)(2,1)S(1)} %pad_maximum_fusion.5), channel_id=1, source_target_pairs={{32,0},{64,32},{96,64},{0,96},{33,1},{65,33},{97,65},{1,97},{34,2}... | collective-permute-start | bytes 677384 | tf_op jit(solution)/shard_map/ppermute | solution.py:322
  13.2 6.7 %copy-start.10 = (f32[288]{0:T(512)S(1)}, f32[288]{0:T(512)}, u32[]{:S(2)}) copy-start(f32[288]{0:T(512)} %param.16) | copy-start | bytes 3460
  19.8 8.1 %collective-permute-start.1 = (bf16[2,28,3,7,96]{4,3,2,1,0:T(8,128)(2,1)}, bf16[2,28,3,7,96]{4,3,2,1,0:T(8,128)(2,1)S(1)}, u32[]{:S(2)}, u32[]{:S(2)}) collective-permute-start(bf16[2,28,3,7,96]{4,3,2,1,0:T(8,128)(2,1)} %pad_maximum_fusion.4), channel_id=1, source_target_pairs={{8,0},{16,8},{24,16},{0,24},{9,1},{17,9},{25,17},{1,25},{10,2},{18... | collective-permute-start | bytes 677384 | tf_op jit(solution)/shard_map/ppermute | solution.py:322
  28.7 8.6 %copy-start.11 = (f32[96]{0:T(128)S(1)}, f32[96]{0:T(128)}, u32[]{:S(2)}) copy-start(f32[96]{0:T(128)} %get-tuple-element.34) | copy-start | bytes 1156
  28.8 8.6 %copy-start.12 = (f32[96]{0:T(128)S(1)}, f32[96]{0:T(128)}, u32[]{:S(2)}) copy-start(f32[96]{0:T(128)} %get-tuple-element.35) | copy-start | bytes 1156
  28.8 8.7 %copy-start.4 = (bf16[96,32]{1,0:T(8,128)(2,1)S(1)}, bf16[96,32]{1,0:T(8,128)(2,1)}, u32[]{:S(2)}) copy-start(bf16[96,32]{1,0:T(8,128)(2,1)} %broadcast_in_dim.18) | copy-start | bytes 18436
  28.8 8.7 %copy-start.8 = (bf16[96,96]{1,0:T(8,128)(2,1)S(1)}, bf16[96,96]{1,0:T(8,128)(2,1)}, u32[]{:S(2)}) copy-start(bf16[96,96]{1,0:T(8,128)(2,1)} %get-tuple-element.28) | copy-start | bytes 55300
  28.8 8.7 %copy-start.9 = (bf16[96,96]{1,0:T(8,128)(2,1)S(1)}, bf16[96,96]{1,0:T(8,128)(2,1)}, u32[]{:S(2)}) copy-start(bf16[96,96]{1,0:T(8,128)(2,1)} %get-tuple-element.29) | copy-start | bytes 55300
  28.8 9.4 %copy-start.6 = (bf16[96,288]{0,1:T(8,128)(2,1)S(1)}, bf16[96,288]{0,1:T(8,128)(2,1)}, u32[]{:S(2)}) copy-start(bf16[96,288]{0,1:T(8,128)(2,1)} %copy.57) | copy-start | bytes 165892
  28.8 10.1 %copy-start.5 = (f32[352,256]{1,0:T(8,128)S(1)}, f32[352,256]{1,0:T(8,128)}, u32[]{:S(2)}) copy-start(f32[352,256]{1,0:T(8,128)} %constant.10.clone) | copy-start | bytes 1081348
  30.7 33.1 %collective-permute-start.2 = (bf16[2,28,28,3,96]{4,0,3,2,1:T(2,128)(2,1)S(1)}, bf16[2,28,28,3,96]{4,0,3,2,1:T(2,128)(2,1)S(1)}, u32[]{:S(2)}, u32[]{:S(2)}) collective-permute-start(bf16[2,28,28,3,96]{4,0,3,2,1:T(2,128)(2,1)S(1)} %copy.51), channel_id=1, source_target_pairs={{1,0},{2,1},{3,2},{4,3},{5,4},{6,5},{7,6},{0,7},{9,8},{10,9},{11,1... | collective-permute-start | bytes 2709512 | tf_op jit(solution)/shard_map/ppermute | solution.py:322
  137.8 6.4 %copy-start.3 = (bf16[16,352,96]{2,1,0:T(8,128)(2,1)S(1)}, bf16[16,352,96]{2,1,0:T(8,128)(2,1)}, u32[]{:S(2)}) copy-start(bf16[16,352,96]{2,1,0:T(8,128)(2,1)} %get-tuple-element.14) | copy-start | bytes 3244036
  145.1 144.5 %collective-permute-start.3 = (bf16[3,28,7,96]{3,2,1,0:T(8,128)(2,1)S(1)}, bf16[3,28,7,96]{3,2,1,0:T(8,128)(2,1)S(1)}, u32[]{:S(2)}, u32[]{:S(2)}) collective-permute-start(bf16[3,28,7,96]{3,2,1,0:T(8,128)(2,1)S(1)} %slice.140), channel_id=1, source_target_pairs={{96,0},{0,32},{32,64},{64,96},{97,1},{1,33},{33,65},{65,97},{98,2}... | collective-permute-start | bytes 338696 | tf_op jit(solution)/shard_map/ppermute | solution.py:322
  289.7 4.9 %collective-permute-start.4 = (bf16[28,3,7,96]{3,2,1,0:T(8,128)(2,1)S(1)}, bf16[28,3,7,96]{3,2,1,0:T(8,128)(2,1)S(1)}, u32[]{:S(2)}, u32[]{:S(2)}) collective-permute-start(bf16[28,3,7,96]{3,2,1,0:T(8,128)(2,1)S(1)} %pad_maximum_fusion.6), channel_id=1, source_target_pairs={{24,0},{0,8},{8,16},{16,24},{25,1},{1,9},{9,17},{17,25},{26,2},{2,... | collective-permute-start | bytes 338696 | tf_op jit(solution)/shard_map/ppermute | solution.py:322
  295.0 7.6 %copy-start.2 = (bf16[28,28,7,96]{3,2,1,0:T(8,128)(2,1)}, bf16[28,28,7,96]{3,2,1,0:T(8,128)(2,1)S(1)}, u32[]{:S(2)}) copy-start(bf16[28,28,7,96]{3,2,1,0:T(8,128)(2,1)S(1)} %fusion.4) | copy-start | bytes 3161092
  295.6 20.3 %collective-permute-start.5 = (bf16[28,28,3,96]{3,1,2,0:T(8,128)(2,1)S(1)}, bf16[28,28,3,96]{3,1,2,0:T(8,128)(2,1)S(1)}, u32[]{:S(2)}, u32[]{:S(2)}) collective-permute-start(bf16[28,28,3,96]{3,1,2,0:T(8,128)(2,1)S(1)} %copy.61), channel_id=1, source_target_pairs={{7,0},{0,1},{1,2},{2,3},{3,4},{4,5},{5,6},{6,7},{15,8},{8,9},{9,10... | collective-permute-start | bytes 1354760 | tf_op jit(solution)/shard_map/ppermute | solution.py:322
  302.6 13.6 %slice-start = ((bf16[28,28,7,96]{3,2,1,0:T(8,128)(2,1)}), bf16[28,28,4,96]{3,2,1,0:T(4,128)(2,1)S(1)}, s32[]{:S(2)}) async-start(bf16[28,28,7,96]{3,2,1,0:T(8,128)(2,1)} %copy-done.2), calls=%async_computation.1 | async-start | bytes 1605632 | tf_op jit(solution)/shard_map/slice | solution.py:355
Sparse Core Ops, SparseCore 0:
  144.4 144.2 all-reduce.4

commit v2 on v1

v2 whole, which is shorter than its diff:
```python
import functools

import jax
import jax.numpy as jnp
import numpy as np
from jax import lax
from jax.experimental import pallas as pl
from jax.experimental.pallas import tpu as pltpu
from jax.sharding import PartitionSpec as P

WIN = 7
SHIFT = 3
TOK = WIN**3
ROWS = 352
LANES = 384
FEATS = 96
HEADS = 3
HDIM = 32
PLANE = 49
WIDTH = 13
TABLE = WIDTH**3
SPREAD = 2304
SQUEEZED = 768
OWN = 196
OTHER = 147
AHEAD = 3
LAG = 2
CHUNK = 56
MESH = pl.DeviceIdType.MESH
FAR = -(2.0**100)
NEVER = -1e30
LOG2E = 1.4426950408889634
SCALE = HDIM**-0.5
F32 = jnp.float32
BF16 = jnp.bfloat16


def nn(a, b):
    return lax.dot_general(a, b, (((1,), (0,)), ((), ())), preferred_element_type=F32)


def nt(a, b):
    return lax.dot_general(a, b, (((1,), (1,)), ((), ())), preferred_element_type=F32)


def token_place(count):
    p = np.arange(count)
    n = np.where(p < OWN, p // 4, (p - OWN) // 3)
    z = np.where(p < OWN, p % 4, 4 + (p - OWN) % 3)
    return n // 7, n % 7, z


def token_late(count):
    return np.stack([(place >= WIN - SHIFT).astype(np.float32) for place in token_place(count)])


def squeeze_ones():
    lane = np.arange(SQUEEZED)
    m = lane - LANES
    own = lane // 28 * 169 + lane % 28 // 4 * 13 + lane % 4
    other = m // 21 * 169 + m % 21 // 3 * 13 + 4 + m % 3
    place = np.where(lane < 364, own, np.where((m >= 0) & (m < 273), other, -1))
    return (np.arange(SPREAD)[:, None] == place[None, :]).astype(np.float32)


def key_features():
    late = token_late(ROWS)
    out = np.zeros((ROWS, 256), np.float32)
    for d in range(3):
        out[:, 96 + 2 * d] = late[d]
        out[:, 97 + 2 * d] = 1 - late[d]
    return out


def query_features():
    late = token_late(LANES)
    out = np.zeros((3, 16, LANES), np.float32)
    for d in range(3):
        out[d, 2 * d] = FAR * (1 - late[d])
        out[d, 2 * d + 1] = FAR * late[d]
    return out


def pieces(x, count):
    out = []
    for _ in range(count):
        piece = x.astype(BF16)
        out.append(piece)
        x = x - piece.astype(F32)
    return out


def expand_table(table_ref, ones_ref, bias_ref, wide_ref, flat_ref):
    for h in range(HEADS):
        row = jnp.broadcast_to(table_ref[h : h + 1, :] * LOG2E, (8, SPREAD))
        row = pltpu.roll(row, 0, 1, stride=1, stride_axis=0)
        for jy in range(WIN):
            moved = pltpu.roll(row, SPREAD - 13 * (6 - jy) - 6, 1)
            for n, piece in enumerate(pieces(moved, 3)):
                wide_ref[n, h * 56 + jy * 8 : h * 56 + jy * 8 + 8, :] = piece.astype(F32)
    total = None
    for n in range(3):
        part = nn(wide_ref[n].astype(BF16), ones_ref[...])
        total = part if total is None else total + part
    flat_ref[...] = total
    lane = lax.broadcasted_iota(jnp.int32, (56, LANES), 1)
    for h in range(HEADS):
        for jx in range(WIN):
            own = pltpu.roll(flat_ref[h * 56 : h * 56 + 56, 0:LANES], (LANES - 28 * (6 - jx)) % LANES, 1)
            other = pltpu.roll(
                flat_ref[h * 56 : h * 56 + 56, LANES:SQUEEZED], (LANES + OWN - 21 * (6 - jx)) % LANES, 1
            )
            both = jnp.where(lane < OWN, own, jnp.where(lane < TOK, other, 0.0))
            for jy in range(WIN):
                n = jx * 7 + jy
                bias_ref[h, pl.ds(4 * n, 4), :] = both[jy * 8 : jy * 8 + 4]
                bias_ref[h, pl.ds(OWN + 3 * n, 3), :] = both[jy * 8 + 4 : jy * 8 + 7]
        bias_ref[h, TOK:ROWS, :] = jnp.full((ROWS - TOK, LANES), NEVER, F32)


def fold_table(sums_ref, ones_ref, wide_ref, flat_ref, put):
    sub = lax.broadcasted_iota(jnp.int32, (8, LANES), 0)
    lane = lax.broadcasted_iota(jnp.int32, (8, LANES), 1)
    for h in range(HEADS):
        for jy in range(WIN):
            own = jnp.zeros((8, LANES), F32)
            other = jnp.zeros((8, LANES), F32)
            for jx in range(WIN):
                n = jx * 7 + jy
                low = sums_ref[h, pl.ds(4 * n, 8), :]
                high = sums_ref[h, pl.ds(OWN + 3 * n - 4, 8), :]
                block = jnp.where(sub < 4, low, high)
                own = own + pltpu.roll(jnp.where(lane < OWN, block, 0.0), 28 * (6 - jx), 1)
                rest = jnp.where((lane >= OWN) & (lane < TOK), block, 0.0)
                other = other + pltpu.roll(rest, (LANES - OWN + 21 * (6 - jx)) % LANES, 1)
            at = h * 56 + jy * 8
            flat_ref[at : at + 8, 0:LANES] = jnp.where(sub < WIN, own, 0.0)
            flat_ref[at : at + 8, LANES:SQUEEZED] = jnp.where(sub < WIN, other, 0.0)
    spread = None
    for piece in pieces(flat_ref[...], 3):
        part = nt(piece, ones_ref[...])
        spread = part if spread is None else spread + part
    wide_ref[0] = spread
    for h in range(HEADS):
        total = jnp.zeros((8, SPREAD), F32)
        for jy in range(WIN):
            block = wide_ref[0, h * 56 + jy * 8 : h * 56 + jy * 8 + 8, :]
            total = total + pltpu.roll(block, 13 * (6 - jy), 1)
        line = jnp.zeros((1, SPREAD), F32)
        for jz in range(WIN):
            line = line + pltpu.roll(total, 6 - jz, 1)[jz : jz + 1]
        for c in range(SPREAD // 128):
            put(384 + h * 18 + c, line[:, c * 128 : c * 128 + 128])


def window_at(t):
    inner = jnp.where(t < 5, t, t - 7)
    edge = t - 5
    side_x = jnp.where(edge < 4, 3, edge - 4)
    side_y = jnp.where(edge < 4, edge, 3)
    is_edge = (t >= 5) & (t < 12)
    return jnp.where(is_edge, side_x, inner // 3), jnp.where(is_edge, side_y, inner % 3)


def whole_kernel(
    x_hbm,
    dy_hbm,
    gain_ref,
    shift_ref,
    table_ref,
    ones_ref,
    w_all_ref,
    w_kv_ref,
    b_col_ref,
    b_kv_ref,
    q_feat_ref,
    w_proj_ref,
    w_qkv_ref,
    out_hbm,
    result_ref,
    bias_ref,
    acc_ref,
    e_ref,
    ds_ref,
    q_ref,
    do_ref,
    ln_ref,
    gq_ref,
    wide_ref,
    flat_ref,
    wq_ref,
    wkv_ref,
    proj_ref,
    rows_ref,
    ext_ref,
    win_ref,
    send_f_ref,
    dyb_ref,
    dx_ref,
    back_f_ref,
    out_ext_ref,
    fwd_send_ref,
    fwd_recv_ref,
    ret_send_ref,
    ret_recv_ref,
    pay_ref,
    near_ref,
    far_ref,
    load_sem,
    halo_send,
    halo_recv,
    fwd_send,
    fwd_recv,
    ret_send,
    ret_recv,
    out_sem,
    edge_send,
    edge_recv,
    near_send,
    near_recv,
    far_send,
    far_recv,
    all_send,
    all_recv,
):
    nx, ny, nz = lax.axis_size("gx"), lax.axis_size("gy"), lax.axis_size("gz")
    gx, gy, gz = lax.axis_index("gx"), lax.axis_index("gy"), lax.axis_index("gz")
    plane = nx * ny
    spot = gx * ny + gy
    cells_x, cells_y = x_hbm.shape[0], x_hbm.shape[1]
    total = (cells_x // WIN) * (cells_y // WIN)

    def peer_z(k):
        return {"gz": lax.rem(gz + k, nz)}

    def peer_xy(k):
        other = lax.rem(spot + k, plane)
        return {"gx": other // ny, "gy": lax.rem(other, ny)}

    barrier = pltpu.get_barrier_semaphore()
    for k in range(1, nz):
        pl.semaphore_signal(barrier, inc=1, device_id=peer_z(k), device_id_type=MESH)
    for k in range(1, plane):
        pl.semaphore_signal(barrier, inc=1, device_id=peer_xy(k), device_id_type=MESH)

    def load(a):
        source = (x_hbm, dy_hbm)[a]
        return pltpu.make_async_copy(
            source, ext_ref.at[a, pl.ds(0, cells_x), pl.ds(0, cells_y)], load_sem.at[a]
        )

    def halo(a, side):
        source = (x_hbm, dy_hbm)[a]
        px, py = ((1, 0), (0, 1), (1, 1))[side]
        from_x = pl.ds(0, SHIFT) if px else pl.ds(0, cells_x)
        from_y = pl.ds(0, SHIFT) if py else pl.ds(0, cells_y)
        to_x = pl.ds(cells_x, SHIFT) if px else pl.ds(0, cells_x)
        to_y = pl.ds(cells_y, SHIFT) if py else pl.ds(0, cells_y)
        return pltpu.make_async_remote_copy(
            src_ref=source.at[from_x, from_y],
            dst_ref=ext_ref.at[a, to_x, to_y],
            send_sem=halo_send.at[a, side],
            recv_sem=halo_recv.at[a, side],
            device_id={"gx": lax.rem(gx + nx - px, nx), "gy": lax.rem(gy + ny - py, ny)},
            device_id_type=MESH,
        )

    def fwd(t):
        return pltpu.make_async_remote_copy(
            src_ref=fwd_send_ref.at[t],
            dst_ref=fwd_recv_ref.at[t],
            send_sem=fwd_send.at[t],
            recv_sem=fwd_recv.at[t],
            device_id=peer_z(nz - 1),
            device_id_type=MESH,
        )

    def ret(t):
        return pltpu.make_async_remote_copy(
            src_ref=ret_send_ref.at[t],
            dst_ref=ret_recv_ref.at[t],
            send_sem=ret_send.at[t],
            recv_sem=ret_recv.at[t],
            device_id=peer_z(1),
            device_id_type=MESH,
        )

    def edge(side):
        px, py = ((1, 0), (0, 1), (1, 1))[side]
        from_x = pl.ds(cells_x, SHIFT) if px else pl.ds(SHIFT, cells_x - SHIFT)
        from_y = pl.ds(cells_y, SHIFT) if py else pl.ds(SHIFT, cells_y - SHIFT)
        to_x = pl.ds(0, SHIFT) if px else pl.ds(SHIFT, cells_x - SHIFT)
        to_y = pl.ds(0, SHIFT) if py else pl.ds(SHIFT, cells_y - SHIFT)
        return pltpu.make_async_remote_copy(
            src_ref=out_ext_ref.at[from_x, from_y],
            dst_ref=out_hbm.at[to_x, to_y],
            send_sem=edge_send.at[side],
            recv_sem=edge_recv.at[side],
            device_id={"gx": lax.rem(gx + px, nx), "gy": lax.rem(gy + py, ny)},
            device_id_type=MESH,
        )

    def store_out():
        inner_x = pl.ds(SHIFT, cells_x - SHIFT)
        inner_y = pl.ds(SHIFT, cells_y - SHIFT)
        return pltpu.make_async_copy(
            out_ext_ref.at[inner_x, inner_y], out_hbm.at[inner_x, inner_y], out_sem
        )

    def near(k):
        return pltpu.make_async_remote_copy(
            src_ref=pay_ref.at[lax.rem(gz + k, nz)],
            dst_ref=near_ref.at[gz],
            send_sem=near_send.at[k],
            recv_sem=near_recv.at[k],
            device_id=peer_z(k),
            device_id_type=MESH,
        )

    def far(k):
        return pltpu.make_async_remote_copy(
            src_ref=far_ref.at[spot],
            dst_ref=far_ref.at[spot],
            send_sem=far_send.at[k],
            recv_sem=far_recv.at[k],
            device_id=peer_xy(k),
            device_id_type=MESH,
        )

    def final(k):
        return pltpu.make_async_remote_copy(
            src_ref=result_ref.at[gz],
            dst_ref=result_ref.at[gz],
            send_sem=all_send.at[k],
            recv_sem=all_recv.at[k],
            device_id=peer_z(k),
            device_id_type=MESH,
        )

    load(0).start()
    load(1).start()
    acc_ref[...] = jnp.zeros_like(acc_ref)
    e_ref[...] = jnp.zeros_like(e_ref)
    ds_ref[...] = jnp.zeros_like(ds_ref)
    q_ref[...] = jnp.zeros_like(q_ref)
    do_ref[...] = jnp.zeros_like(do_ref)
    wq_ref[...] = jnp.zeros_like(wq_ref)
    wkv_ref[...] = jnp.zeros_like(wkv_ref)
    proj_ref[...] = jnp.zeros_like(proj_ref)
    rows_ref[...] = jnp.zeros_like(rows_ref)
    gq_ref[...] = jnp.zeros_like(gq_ref)
    ln_ref[...] = jnp.zeros_like(ln_ref)
    dyb_ref[...] = jnp.zeros_like(dyb_ref)
    send_f_ref[...] = jnp.zeros_like(send_f_ref)
    pay_ref[...] = jnp.zeros_like(pay_ref)
    for t in range(total):
        dx_ref[t, 0:8, :] = jnp.zeros((8, FEATS), F32)
        dx_ref[t, 360:368, :] = jnp.zeros((8, FEATS), F32)
    pl.semaphore_wait(barrier, nz - 1 + plane - 1)
    for a in range(2):
        for side in range(3):
            halo(a, side).start()
    load(0).wait()
    load(1).wait()

    def gather(t):
        wx, wy = window_at(t)
        for a in range(2):
            for ix in range(WIN):
                for iy in range(WIN):
                    n = ix * WIN + iy
                    tile = ext_ref[a, wx * WIN + SHIFT + ix, wy * WIN + SHIFT + iy].astype(F32)
                    win_ref[t, a, pl.ds(4 * n, 4), :] = tile[3:7]
                    send_f_ref[pl.ds(3 * n, 3), :] = tile[0:3]
            fwd_send_ref[t, a] = send_f_ref[...].astype(BF16)
        fwd(t).start()

    def first_gather(t, carry):
        gather(t)
        return carry

    lax.fori_loop(0, AHEAD, first_gather, 0)
    expand_table(table_ref, ones_ref, bias_ref, wide_ref, flat_ref)

    def compute(t):
        wx, wy = window_at(t)
        last_x = (gx == nx - 1) & (wx == cells_x // WIN - 1)
        last_y = (gy == ny - 1) & (wy == cells_y // WIN - 1)
        last_z = gz == nz - 1
        fwd(t).wait_recv()
        for a in range(2):
            win_ref[t, a, OWN:ROWS, :] = fwd_recv_ref[t, a].astype(F32)[0 : ROWS - OWN]
        x = win_ref[t, 0]
        mean = jnp.mean(x, -1, keepdims=True)
        centered = x - mean
        rstd = lax.rsqrt(jnp.mean(centered * centered, -1, keepdims=True) + 1e-05)
        xhat = centered * rstd
        ln_ref[0:ROWS, :] = (xhat * gain_ref[...] + shift_ref[...]).astype(BF16)

        across = nt(w_all_ref[...], ln_ref[...])
        q_t = ((across[0:96] + b_col_ref[0:96]) * (SCALE * LOG2E)).astype(BF16)
        k_t = (across[96:192] + b_col_ref[96:192]).astype(BF16)
        v_t = (across[192:288] + b_col_ref[192:288]).astype(BF16)
        ln_t = across[288:384].astype(BF16)
        marks = (
            q_feat_ref[0] * last_x.astype(F32)
            + q_feat_ref[1] * last_y.astype(F32)
            + q_feat_ref[2] * last_z.astype(F32)
        ).astype(BF16)
        for h in range(HEADS):
            q_ref[h * HDIM : (h + 1) * HDIM, h * LANES : (h + 1) * LANES] = q_t[h * HDIM : (h + 1) * HDIM]
            q_ref[96:112, h * LANES : (h + 1) * LANES] = marks
        kv = nn(ln_ref[0:ROWS, :], w_kv_ref[...]) + b_kv_ref[...]
        k = kv[:, 0:128].astype(BF16)
        v = kv[:, 128:256].astype(BF16)
        dyb_ref[0:ROWS, :] = win_ref[t, 1].astype(BF16)
        dy = dyb_ref[...]
        do_t = nt(w_proj_ref[...], dy)

        att = []
        for h in range(HEADS):
            inverse = []
            for c in range(3):
                at = pl.ds(h * LANES + c * 128, 128)
                s = nn(k, q_ref[:, at]) + bias_ref[h, :, pl.ds(c * 128, 128)]
                e = jnp.exp2(s - jnp.max(s, 0, keepdims=True))
                inv = 1.0 / jnp.sum(e, 0, keepdims=True)
                inverse.append(inv)
                e_ref[0:ROWS, at] = e.astype(BF16)
                do_ref[h * HDIM : (h + 1) * HDIM, at] = (
                    do_t[h * HDIM : (h + 1) * HDIM, c * 128 : c * 128 + 128] * inv
                ).astype(BF16)
                dp = nn(v, do_ref[:, at])
                ds = e * (dp - jnp.sum(e * dp, 0, keepdims=True) * inv)
                acc_ref[h, :, pl.ds(c * 128, 128)] += ds
                ds_ref[0:ROWS, at] = ds.astype(BF16)
            at = pl.ds(h * LANES, LANES)
            inverse = jnp.concatenate(inverse, 1)
            o_t = nn(v_t[h * HDIM : (h + 1) * HDIM], e_ref[:, at]) * inverse
            att.append(o_t.astype(BF16))
            gq_ref[h * HDIM : (h + 1) * HDIM, :] = nn(k_t[h * HDIM : (h + 1) * HDIM], ds_ref[:, at]) * SCALE
        att = jnp.concatenate(att, 0)
        proj_ref[...] += nn(att, dy)
        grad_v = nt(e_ref[0:ROWS, :], do_ref[...])
        grad_k = nt(ds_ref[0:ROWS, :], q_ref[0:96, :]) * (1.0 / LOG2E)
        gq = gq_ref[...]
        wq_ref[0:96, 0:96] += nn(gq[0:96].astype(BF16), ln_ref[...])
        turned = gq.T[0:ROWS, 0:96]
        grad_q = turned.astype(BF16)
        grad_v = grad_v[:, 0:96]
        k_b = grad_k.astype(BF16)
        v_b = grad_v.astype(BF16)
        wkv_ref[:, 0:96] += nn(ln_t[:, 0:ROWS], k_b)
        wkv_ref[:, 128:224] += nn(ln_t[:, 0:ROWS], v_b)
        grad_in = (
            nt(grad_q, w_qkv_ref[:, 0:96])
            + nt(k_b, w_qkv_ref[:, 128:224])
            + nt(v_b, w_qkv_ref[:, 256:352])
        )
        for n, term in enumerate((turned, grad_k, grad_v, xhat * grad_in, grad_in)):
            rows_ref[n] += jnp.sum(term.reshape(ROWS // 8, 8, 96), 0)
        dhat = grad_in * gain_ref[...]
        first = jnp.mean(dhat, -1, keepdims=True)
        second = jnp.mean(dhat * xhat, -1, keepdims=True)
        dx_ref[t, 8 : 8 + ROWS, :] = win_ref[t, 1] + rstd * (dhat - first - xhat * second)
        ret_send_ref[t] = dx_ref[t, 8 + OWN : 8 + OWN + 160, :].astype(BF16)
        ret(t).start()

    sub = lax.broadcasted_iota(jnp.int32, (8, FEATS), 0)

    def merge(t):
        wx, wy = window_at(t)
        ret(t).wait_recv()
        back_f_ref[...] = ret_recv_ref[t].astype(F32)
        for ix in range(WIN):
            for iy in range(WIN):
                n = ix * WIN + iy
                low = back_f_ref[pl.ds(3 * n, 8), :]
                high = dx_ref[t, pl.ds(5 + 4 * n, 8), :]
                tile = jnp.where(sub < SHIFT, low, high).astype(BF16)
                out_ext_ref[wx * WIN + SHIFT + ix, wy * WIN + SHIFT + iy] = tile[0:7]

    def step(t, carry):
        @pl.when(t == 5 - AHEAD)
        def _():
            for a in range(2):
                for side in range(3):
                    halo(a, side).wait_recv()

        @pl.when(t + AHEAD < total)
        def _():
            gather(t + AHEAD)

        compute(t)

        @pl.when(t >= LAG)
        def _():
            merge(t - LAG)

        return carry

    lax.fori_loop(0, total, step, 0)

    def put(row, value):
        while value.shape[0]:
            chunk, at = divmod(row, CHUNK)
            count = min(CHUNK - at, value.shape[0])
            pay_ref[chunk, at : at + count, 0 : value.shape[1]] = value[0:count]
            value = value[count:]
            row += count

    put(0, wq_ref[...].T[0:96, 0:96])
    put(96, wkv_ref[:, 0:96])
    put(192, wkv_ref[:, 128:224])
    put(288, proj_ref[...])
    for n in range(5):
        put(438 + n, jnp.sum(rows_ref[n], 0, keepdims=True))
    fold_table(acc_ref, ones_ref, wide_ref, flat_ref, put)
    for k in range(1, nz):
        near(k).start()
    near_ref[gz] = pay_ref[gz]

    def last_merge(t, carry):
        merge(t)
        return carry

    lax.fori_loop(total - LAG, total, last_merge, 0)
    store_out().start()
    for side in range(3):
        edge(side).start()
    for k in range(1, nz):
        near(k).wait_recv()
    far_ref[spot] = jnp.sum(near_ref[...], 0)
    for k in range(1, plane):
        far(k).start()
    for k in range(1, plane):
        far(k).wait_recv()
    result_ref[gz] = jnp.sum(far_ref[...], 0)
    for k in range(1, nz):
        final(k).start()
    store_out().wait()
    for side in range(3):
        edge(side).wait()
    for a in range(2):
        for side in range(3):
            halo(a, side).wait_send()

    def drain(t, carry):
        fwd(t).wait_send()
        ret(t).wait_send()
        return carry

    lax.fori_loop(0, total, drain, 0)
    for k in range(1, nz):
        near(k).wait_send()
    for k in range(1, plane):
        far(k).wait_send()
    for k in range(1, nz):
        final(k).wait()


def whole_call(inputs, d_out, gain, shift, table, w_qkv, b_qkv, w_proj):
    cells_x, cells_y, cells_z, _ = inputs.shape
    count = (cells_x // WIN) * (cells_y // WIN)
    nz, plane = lax.axis_size("gz"), lax.axis_size("gx") * lax.axis_size("gy")
    ones = jnp.asarray(squeeze_ones(), BF16)
    w_t = w_qkv.T
    w_all = jnp.concatenate([w_t, jnp.eye(96, dtype=BF16)], 0)
    gap = jnp.zeros((96, 32), BF16)
    w_k, w_v = w_qkv[:, 96:192], w_qkv[:, 192:288]
    w_kv = jnp.concatenate([w_k, gap, w_v, gap], 1)
    w_back = jnp.concatenate([w_qkv[:, 0:96], gap, w_k, gap, w_v, gap], 1)
    gap_b = jnp.zeros((32,), F32)
    b_row = jnp.concatenate([b_qkv[96:192], gap_b, b_qkv[192:288], gap_b])
    b_kv = jnp.asarray(key_features()) + b_row[None, :]
    b_col = b_qkv[:, None]
    table = jnp.pad(table, ((0, 5), (0, SPREAD - TABLE)))
    consts = (gain[None, :], shift[None, :], table, ones, w_all, w_kv, b_col, b_kv)
    consts += (jnp.asarray(query_features()), w_proj, w_back)
    outs = (
        jax.ShapeDtypeStruct(inputs.shape, BF16),
        jax.ShapeDtypeStruct((nz, CHUNK, 128), F32),
    )
    anywhere = pl.BlockSpec(memory_space=pl.ANY)
    inside = pl.BlockSpec(memory_space=pltpu.VMEM)
    dma = pltpu.SemaphoreType.DMA
    return pl.pallas_call(
        whole_kernel,
        in_specs=[anywhere] * 2 + [inside] * len(consts),
        out_specs=[anywhere, inside],
        out_shape=outs,
        scratch_shapes=[
            pltpu.VMEM((HEADS, ROWS, LANES), F32),
            pltpu.VMEM((HEADS, ROWS, LANES), F32),
            pltpu.VMEM((LANES, HEADS * LANES), BF16),
            pltpu.VMEM((LANES, HEADS * LANES), BF16),
            pltpu.VMEM((128, HEADS * LANES), BF16),
            pltpu.VMEM((128, HEADS * LANES), BF16),
            pltpu.VMEM((LANES, FEATS), BF16),
            pltpu.VMEM((128, LANES), F32),
            pltpu.VMEM((3, HEADS * 56, SPREAD), F32),
            pltpu.VMEM((HEADS * 56, SQUEEZED), F32),
            pltpu.VMEM((128, 128), F32),
            pltpu.VMEM((96, 256), F32),
            pltpu.VMEM((96, 96), F32),
            pltpu.VMEM((5, 8, 96), F32),
            pltpu.VMEM((2, cells_x + SHIFT, cells_y + SHIFT, cells_z, FEATS), BF16),
            pltpu.VMEM((count, 2, ROWS, FEATS), F32),
            pltpu.VMEM((160, FEATS), F32),
            pltpu.VMEM((LANES, FEATS), BF16),
            pltpu.VMEM((count, 368, FEATS), F32),
            pltpu.VMEM((160, FEATS), F32),
            pltpu.VMEM((cells_x + SHIFT, cells_y + SHIFT, cells_z, FEATS), BF16),
            pltpu.VMEM((count, 2, 160, FEATS), BF16),
            pltpu.VMEM((count, 2, 160, FEATS), BF16),
            pltpu.VMEM((count, 160, FEATS), BF16),
            pltpu.VMEM((count, 160, FEATS), BF16),
            pltpu.VMEM((nz, CHUNK, 128), F32),
            pltpu.VMEM((nz, CHUNK, 128), F32),
            pltpu.VMEM((plane, CHUNK, 128), F32),
            dma((2,)),
            dma((2, 3)),
            dma((2, 3)),
            dma((count,)),
            dma((count,)),
            dma((count,)),
            dma((count,)),
            dma,
            dma((3,)),
            dma((3,)),
            dma((nz,)),
            dma((nz,)),
            dma((plane,)),
            dma((plane,)),
            dma((nz,)),
            dma((nz,)),
        ],
        compiler_params=pltpu.CompilerParams(
            vmem_limit_bytes=56 << 20, collective_id=0, has_side_effects=True
        ),
    )(inputs, d_out, *consts)


def shards(inputs, d_out, gain, shift, w_qkv, b_qkv, w_proj, rel_bias):
    field, sums = whole_call(inputs, d_out, gain, shift, rel_bias, w_qkv, b_qkv, w_proj)
    count = inputs.size // FEATS * lax.axis_size("gx") * lax.axis_size("gy") * lax.axis_size("gz")
    sums = sums.reshape(-1, 128) * float(count) ** -0.5
    weight = jnp.concatenate([sums[0:96, :96], sums[96:192, :96], sums[192:288, :96]], 1)
    proj = sums[288:384, :96]
    rel = sums[384:438].reshape(HEADS, SPREAD)[:, :TABLE]
    bias = sums[438:441, :96].reshape(-1)
    return field, weight, bias, proj, rel, sums[441, :96], sums[442, :96]


def solution(mesh):
    placed = (P("gx", "gy", "gz", None), P("gx", "gy", "gz", None), P(), P(), P(), P(), P(), P())
    return jax.shard_map(
        shards,
        mesh=mesh,
        in_specs=placed,
        out_specs=(P("gx", "gy", "gz", None), P(), P(), P(), P(), P(), P()),
        check_vma=False,
    )
```

time: 326 us -> 121 us (0.37)
  waiting for transfers between devices: 187 us -> 0 us
  Pallas kernels: 66.7 us -> 103 us
  other arithmetic: 20.1 us -> 4.96 us
  between operations: 14.4 us -> 0.67 us
  starting transfers between devices: 13.1 us -> 0 us
  local copies, waits for them, and re-layouts: 23.6 us -> 11.5 us
    psum x1 -> x0, waiting for transfers between devices: 142 us -> none  [in_one(): so_far = lax.psum(jnp.concatenate([a.ravel() for a in arrays]), axis)]
    ppermute x6 -> x0, waiting for transfers between devices: 45 us -> none  [shifted(): return lax.ppermute(block, axis, route)]
    pallas_call x1, Pallas kernels: 66.7 us -> 103 us  [whole_call(): pl.pallas_call(whole_kernel, in_specs=[anywhere] * 2 + [inside] * len(con...]
    ppermute x6 -> x0, starting transfers between devices: 13 us -> none  [shifted(): return lax.ppermute(block, axis, route)]
    concatenate x11 -> x4, other arithmetic: 10.4 us -> 2.24 us  [the longest x1 0.78 us: shards(): jnp.concatenate([sums[0:96, :96], sums[96:192, :96], sums[192:288, :96]], 1)]
    mul x5 -> x1, other arithmetic: 5.19 us -> 0.96 us  [shards(): sums = sums.reshape(-1, 128) * float(count) ** (-0.5)]
    slice x13 -> x5, local copies, waits for them, and re-layouts: 5.88 us -> 2.43 us  [the longest x1 0.96 us: whole_call(): w_back = jnp.concatenate([w_qkv[:, 0:96], gap, w_k, gap, w_v, gap], 1)]
  transfers between devices with their start and end apart: 7 -> 0, of which waited for: 5 -> 0; matrix products, arithmetic and copies ran while one was open for 7% -> 0% of each run, Pallas kernels for 0% -> 0%
where the time goes in v2:
time: 121 us; the launch traced here: 120 us
  Pallas kernels  103 us (85%)
  local copies, waits for them, and re-layouts  11.5 us (10%)
  other arithmetic  4.96 us (4%)
    pallas_call x1, Pallas kernels, whole_call(): pl.pallas_call(whole_kernel, in_specs=[anywhere] * 2 + [inside] * len(con...  103 us
    unnamed x2, local copies, waits for them, and re-layouts  3.67 us

profile of v2, /device:TPU:0, one launch (start us, length us, event | category | flops | bytes accessed | tf_op | source)
XLA Modules:
  0.0 120.5 jit_solution(5602160051812654699)
XLA Ops:
  0.6 0.8 fusion.3
  1.5 0.1 pad_maximum_fusion.3
  1.6 1.4 %pad.4.table_ref = f32[8,2304]{1,0:T(8,128)} pad(f32[3,2197]{1,0:T(4,128)} %param.18, f32[]{:T(128)} %constant.6.clone.1), padding=0_5x0_107 | pad | bytes 100096 | tf_op jit(solution)/shard_map/jit(_pad)/pad | solution.py:577
  3.0 1.0 copy.19
  4.0 0.7 pad_maximum_fusion.1.w_all_ref
  4.6 1.0 fusion.2
  5.6 0.8 concatenate.18.w_qkv_ref
  6.4 0.7 pad_maximum_fusion.2.w_kv_ref
  7.1 1.4 %broadcast_in_dim.21.b_col_ref = f32[288,1]{1,0:T(8,128)} reshape(f32[288]{0:T(512)} %param.16) | data formatting | bytes 2304 | tf_op jit(solution)/shard_map/broadcast_in_dim | solution.py:576
  8.5 1.7 %broadcast_add_fusion.b_kv_ref = f32[352,256]{1,0:T(8,128)} fusion(f32[352,256]{1,0:T(8,128)} %constant.15.clone, f32[256]{0:T(256)S(1)} %pad_maximum_fusion.3), kind=kLoop, calls=%fused_computation | loop fusion | flops 90112 | bytes 721920 | tf_op jit(solution)/shard_map/add | solution.py:575
  10.3 103.3 %shard_map.162 = (bf16[28,28,7,96]{3,2,1,0:T(8,128)(2,1)}, f32[8,56,128]{2,1,0:T(8,128)}) custom-call(bf16[28,28,7,96]{3,2,1,0:T(8,128)(2,1)} %x_hbm.1, bf16[28,28,7,96]{3,2,1,0:T(8,128)(2,1)} %dy_hbm.1, f32[1,96]{1,0:T(1,128)} %bitcast.15, f32[1,96]{1,0:T(1,128)} %bitcast.16, f32[8,2304]{1,0:T(8,128)} %pad.4.table_ref, ...), custom_call_target="tpu_custom_call" | custom-call | tf_op jit(solution)/shard_map/pallas_call | solution.py:587
  113.6 1.0 broadcast_multiply_fusion
  114.5 0.5 slice_bitcast_fusion
  115.1 0.7 reshape.24
  115.7 0.6 fusion.1
  116.4 0.6 reshape.25
  117.0 0.8 pad_maximum_fusion
  117.8 2.7 %copy.22 = bf16[28,28,7,96]{3,2,1,0:T(8,128)(2,1)} copy(bf16[28,28,7,96]{3,2,1,0:T(8,128)(2,1)} %get-tuple-element.29) | data formatting | bytes 2107392
  (5 shorter events, 0.0 us)

commit v3 on v2

--- a/solution.py
+++ b/solution.py
@@ -25,7 +25,7 @@
 OTHER = 147
 AHEAD = 3
 LAG = 2
-CHUNK = 56
+QUAD = 4
 MESH = pl.DeviceIdType.MESH
 FAR = -(2.0**100)
 NEVER = -1e30
@@ -113,9 +113,9 @@
             both = jnp.where(lane < OWN, own, jnp.where(lane < TOK, other, 0.0))
             for jy in range(WIN):
                 n = jx * 7 + jy
-                bias_ref[h, pl.ds(4 * n, 4), :] = both[jy * 8 : jy * 8 + 4]
-                bias_ref[h, pl.ds(OWN + 3 * n, 3), :] = both[jy * 8 + 4 : jy * 8 + 7]
-        bias_ref[h, TOK:ROWS, :] = jnp.full((ROWS - TOK, LANES), NEVER, F32)
+                bias_ref[pl.ds(4 * n, 4), h * LANES : (h + 1) * LANES] = both[jy * 8 : jy * 8 + 4]
+                bias_ref[pl.ds(OWN + 3 * n, 3), h * LANES : (h + 1) * LANES] = both[jy * 8 + 4 : jy * 8 + 7]
+        bias_ref[TOK:ROWS, h * LANES : (h + 1) * LANES] = jnp.full((ROWS - TOK, LANES), NEVER, F32)
 
 
 def fold_table(sums_ref, ones_ref, wide_ref, flat_ref, put):
@@ -127,8 +127,8 @@
             other = jnp.zeros((8, LANES), F32)
             for jx in range(WIN):
                 n = jx * 7 + jy
-                low = sums_ref[h, pl.ds(4 * n, 8), :]
-                high = sums_ref[h, pl.ds(OWN + 3 * n - 4, 8), :]
+                low = sums_ref[pl.ds(4 * n, 8), h * LANES : (h + 1) * LANES]
+                high = sums_ref[pl.ds(OWN + 3 * n - 4, 8), h * LANES : (h + 1) * LANES]
                 block = jnp.where(sub < 4, low, high)
                 own = own + pltpu.roll(jnp.where(lane < OWN, block, 0.0), 28 * (6 - jx), 1)
                 rest = jnp.where((lane >= OWN) & (lane < TOK), block, 0.0)
@@ -169,15 +169,19 @@
     shift_ref,
     table_ref,
     ones_ref,
+    w_raw_ref,
+    b_raw_ref,
+    k_feat_ref,
+    q_feat_ref,
+    w_proj_ref,
+    out_hbm,
+    result_ref,
     w_all_ref,
     w_kv_ref,
     b_col_ref,
     b_kv_ref,
-    q_feat_ref,
-    w_proj_ref,
     w_qkv_ref,
-    out_hbm,
-    result_ref,
+    wide_table_ref,
     bias_ref,
     acc_ref,
     e_ref,
@@ -205,6 +209,7 @@
     ret_recv_ref,
     pay_ref,
     near_ref,
+    part_ref,
     far_ref,
     load_sem,
     halo_send,
@@ -220,6 +225,8 @@
     near_recv,
     far_send,
     far_recv,
+    share_send,
+    share_recv,
     all_send,
     all_recv,
 ):
@@ -319,10 +326,20 @@
 
     def far(k):
         return pltpu.make_async_remote_copy(
-            src_ref=far_ref.at[spot],
+            src_ref=part_ref.at[lax.rem(spot + k, plane)],
             dst_ref=far_ref.at[spot],
             send_sem=far_send.at[k],
             recv_sem=far_recv.at[k],
+            device_id=peer_xy(k),
+            device_id_type=MESH,
+        )
+
+    def share(k):
+        return pltpu.make_async_remote_copy(
+            src_ref=result_ref.at[gz, spot],
+            dst_ref=result_ref.at[gz, spot],
+            send_sem=share_send.at[k],
+            recv_sem=share_recv.at[k],
             device_id=peer_xy(k),
             device_id_type=MESH,
         )
@@ -356,6 +373,28 @@
     for t in range(total):
         dx_ref[t, 0:8, :] = jnp.zeros((8, FEATS), F32)
         dx_ref[t, 360:368, :] = jnp.zeros((8, FEATS), F32)
+    gq_ref[0:96, 0:288] = w_raw_ref[...].astype(F32)
+    wide_w = gq_ref[...]
+    lane = lax.broadcasted_iota(jnp.int32, (96, 128), 1)
+    w_all_ref[0:288, :] = wide_w.T[0:288, 0:96].astype(BF16)
+    eye = lax.broadcasted_iota(jnp.int32, (96, 96), 0) == lax.broadcasted_iota(jnp.int32, (96, 96), 1)
+    w_all_ref[288:384, :] = eye.astype(F32).astype(BF16)
+    turns = [wide_w if n == 0 else pltpu.roll(wide_w, LANES - 96 * n, 1) for n in range(3)]
+    for n in range(3):
+        piece = jnp.where(lane < FEATS, turns[n][0:96, 0:128], 0.0).astype(BF16)
+        w_qkv_ref[:, n * 128 : n * 128 + 128] = piece
+        if n:
+            w_kv_ref[:, n * 128 - 128 : n * 128] = piece
+    gq_ref[...] = jnp.zeros_like(gq_ref)
+    gq_ref[:, 0:288] = jnp.broadcast_to(b_raw_ref[...], (128, 288))
+    wide_b = gq_ref[...]
+    b_col_ref[...] = wide_b.T
+    for n in (1, 2):
+        piece = jnp.where(lane[0:1] < FEATS, pltpu.roll(wide_b, LANES - 96 * n, 1)[0:1, 0:128], 0.0)
+        b_kv_ref[:, n * 128 - 128 : n * 128] = k_feat_ref[:, n * 128 - 128 : n * 128] + piece
+    gq_ref[...] = jnp.zeros_like(gq_ref)
+    wide_table_ref[...] = jnp.zeros_like(wide_table_ref)
+    wide_table_ref[0:HEADS, 0:TABLE] = table_ref[...]
     pl.semaphore_wait(barrier, nz - 1 + plane - 1)
     for a in range(2):
         for side in range(3):
@@ -380,7 +419,7 @@
         return carry
 
     lax.fori_loop(0, AHEAD, first_gather, 0)
-    expand_table(table_ref, ones_ref, bias_ref, wide_ref, flat_ref)
+    expand_table(wide_table_ref, ones_ref, bias_ref, wide_ref, flat_ref)
 
     def compute(t):
         wx, wy = window_at(t)
@@ -398,9 +437,9 @@
         ln_ref[0:ROWS, :] = (xhat * gain_ref[...] + shift_ref[...]).astype(BF16)
 
         across = nt(w_all_ref[...], ln_ref[...])
-        q_t = ((across[0:96] + b_col_ref[0:96]) * (SCALE * LOG2E)).astype(BF16)
-        k_t = (across[96:192] + b_col_ref[96:192]).astype(BF16)
-        v_t = (across[192:288] + b_col_ref[192:288]).astype(BF16)
+        q_t = ((across[0:96] + b_col_ref[0:96, 0:1]) * (SCALE * LOG2E)).astype(BF16)
+        k_t = (across[96:192] + b_col_ref[96:192, 0:1]).astype(BF16)
+        v_t = (across[192:288] + b_col_ref[192:288, 0:1]).astype(BF16)
         ln_t = across[288:384].astype(BF16)
         marks = (
             q_feat_ref[0] * last_x.astype(F32)
@@ -417,27 +456,22 @@
         dy = dyb_ref[...]
         do_t = nt(w_proj_ref[...], dy)
 
+        for h in range(HEADS):
+            do_ref[h * HDIM : (h + 1) * HDIM, h * LANES : (h + 1) * LANES] = do_t[h * HDIM : (h + 1) * HDIM].astype(BF16)
+        for u in range(0, HEADS * LANES, 256):
+            at = pl.ds(u, min(256, HEADS * LANES - u))
+            s = nn(k, q_ref[:, at]) + bias_ref[:, at]
+            dp = nn(v, do_ref[:, at])
+            e = jnp.exp2(s - jnp.max(s, 0, keepdims=True))
+            e = e * (1.0 / jnp.sum(e, 0, keepdims=True))
+            e_ref[0:ROWS, at] = e.astype(BF16)
+            ds = e * (dp - jnp.sum(e * dp, 0, keepdims=True))
+            acc_ref[:, at] += ds
+            ds_ref[0:ROWS, at] = ds.astype(BF16)
         att = []
         for h in range(HEADS):
-            inverse = []
-            for c in range(3):
-                at = pl.ds(h * LANES + c * 128, 128)
-                s = nn(k, q_ref[:, at]) + bias_ref[h, :, pl.ds(c * 128, 128)]
-                e = jnp.exp2(s - jnp.max(s, 0, keepdims=True))
-                inv = 1.0 / jnp.sum(e, 0, keepdims=True)
-                inverse.append(inv)
-                e_ref[0:ROWS, at] = e.astype(BF16)
-                do_ref[h * HDIM : (h + 1) * HDIM, at] = (
-                    do_t[h * HDIM : (h + 1) * HDIM, c * 128 : c * 128 + 128] * inv
-                ).astype(BF16)
-                dp = nn(v, do_ref[:, at])
-                ds = e * (dp - jnp.sum(e * dp, 0, keepdims=True) * inv)
-                acc_ref[h, :, pl.ds(c * 128, 128)] += ds
-                ds_ref[0:ROWS, at] = ds.astype(BF16)
             at = pl.ds(h * LANES, LANES)
-            inverse = jnp.concatenate(inverse, 1)
-            o_t = nn(v_t[h * HDIM : (h + 1) * HDIM], e_ref[:, at]) * inverse
-            att.append(o_t.astype(BF16))
+            att.append(nn(v_t[h * HDIM : (h + 1) * HDIM], e_ref[:, at]).astype(BF16))
             gq_ref[h * HDIM : (h + 1) * HDIM, :] = nn(k_t[h * HDIM : (h + 1) * HDIM], ds_ref[:, at]) * SCALE
         att = jnp.concatenate(att, 0)
         proj_ref[...] += nn(att, dy)
@@ -501,41 +535,55 @@
 
     lax.fori_loop(0, total, step, 0)
 
+    block = plane * QUAD
+
     def put(row, value):
         while value.shape[0]:
-            chunk, at = divmod(row, CHUNK)
-            count = min(CHUNK - at, value.shape[0])
-            pay_ref[chunk, at : at + count, 0 : value.shape[1]] = value[0:count]
+            at = row % QUAD
+            count = min(QUAD - at, value.shape[0])
+            pay_ref[row // block, row % block // QUAD, at : at + count, 0 : value.shape[1]] = value[0:count]
             value = value[count:]
             row += count
 
+    table_block = 384 // block
     put(0, wq_ref[...].T[0:96, 0:96])
     put(96, wkv_ref[:, 0:96])
     put(192, wkv_ref[:, 128:224])
     put(288, proj_ref[...])
+    for k in range(1, nz):
+        @pl.when(lax.rem(gz + k, nz) != table_block)
+        def _():
+            near(k).start()
+
+    def last_merge(t, carry):
+        merge(t)
+        return carry
+
+    lax.fori_loop(total - LAG, total, last_merge, 0)
+    store_out().start()
+    for side in range(3):
+        edge(side).start()
     for n in range(5):
         put(438 + n, jnp.sum(rows_ref[n], 0, keepdims=True))
     fold_table(acc_ref, ones_ref, wide_ref, flat_ref, put)
     for k in range(1, nz):
-        near(k).start()
+        @pl.when(lax.rem(gz + k, nz) == table_block)
+        def _():
+            near(k).start()
     near_ref[gz] = pay_ref[gz]
-
-    def last_merge(t, carry):
-        merge(t)
-        return carry
-
-    lax.fori_loop(total - LAG, total, last_merge, 0)
-    store_out().start()
-    for side in range(3):
-        edge(side).start()
     for k in range(1, nz):
         near(k).wait_recv()
-    far_ref[spot] = jnp.sum(near_ref[...], 0)
+    part_ref[...] = jnp.sum(near_ref[...], 0)
     for k in range(1, plane):
         far(k).start()
+    far_ref[spot] = part_ref[spot]
     for k in range(1, plane):
         far(k).wait_recv()
-    result_ref[gz] = jnp.sum(far_ref[...], 0)
+    result_ref[gz, spot] = jnp.sum(far_ref[...], 0)
+    for k in range(1, plane):
+        share(k).start()
+    for k in range(1, plane):
+        share(k).wait_recv()
     for k in range(1, nz):
         final(k).start()
     store_out().wait()
@@ -555,6 +603,7 @@
         near(k).wait_send()
     for k in range(1, plane):
         far(k).wait_send()
+        share(k).wait_send()
     for k in range(1, nz):
         final(k).wait()
 
@@ -564,22 +613,11 @@
     count = (cells_x // WIN) * (cells_y // WIN)
     nz, plane = lax.axis_size("gz"), lax.axis_size("gx") * lax.axis_size("gy")
     ones = jnp.asarray(squeeze_ones(), BF16)
-    w_t = w_qkv.T
-    w_all = jnp.concatenate([w_t, jnp.eye(96, dtype=BF16)], 0)
-    gap = jnp.zeros((96, 32), BF16)
-    w_k, w_v = w_qkv[:, 96:192], w_qkv[:, 192:288]
-    w_kv = jnp.concatenate([w_k, gap, w_v, gap], 1)
-    w_back = jnp.concatenate([w_qkv[:, 0:96], gap, w_k, gap, w_v, gap], 1)
-    gap_b = jnp.zeros((32,), F32)
-    b_row = jnp.concatenate([b_qkv[96:192], gap_b, b_qkv[192:288], gap_b])
-    b_kv = jnp.asarray(key_features()) + b_row[None, :]
-    b_col = b_qkv[:, None]
-    table = jnp.pad(table, ((0, 5), (0, SPREAD - TABLE)))
-    consts = (gain[None, :], shift[None, :], table, ones, w_all, w_kv, b_col, b_kv)
-    consts += (jnp.asarray(query_features()), w_proj, w_back)
+    consts = (gain[None, :], shift[None, :], table, ones, w_qkv, b_qkv[None, :])
+    consts += (jnp.asarray(key_features()), jnp.asarray(query_features()), w_proj)
     outs = (
         jax.ShapeDtypeStruct(inputs.shape, BF16),
-        jax.ShapeDtypeStruct((nz, CHUNK, 128), F32),
+        jax.ShapeDtypeStruct((nz, plane, QUAD, 128), F32),
     )
     anywhere = pl.BlockSpec(memory_space=pl.ANY)
     inside = pl.BlockSpec(memory_space=pltpu.VMEM)
@@ -590,8 +628,14 @@
         out_specs=[anywhere, inside],
         out_shape=outs,
         scratch_shapes=[
-            pltpu.VMEM((HEADS, ROWS, LANES), F32),
-            pltpu.VMEM((HEADS, ROWS, LANES), F32),
+            pltpu.VMEM((LANES, FEATS), BF16),
+            pltpu.VMEM((96, 256), BF16),
+            pltpu.VMEM((LANES, 128), F32),
+            pltpu.VMEM((ROWS, 256), F32),
+            pltpu.VMEM((96, LANES), BF16),
+            pltpu.VMEM((8, SPREAD), F32),
+            pltpu.VMEM((ROWS, HEADS * LANES), F32),
+            pltpu.VMEM((ROWS, HEADS * LANES), F32),
             pltpu.VMEM((LANES, HEADS * LANES), BF16),
             pltpu.VMEM((LANES, HEADS * LANES), BF16),
             pltpu.VMEM((128, HEADS * LANES), BF16),
@@ -615,9 +659,10 @@
             pltpu.VMEM((count, 2, 160, FEATS), BF16),
             pltpu.VMEM((count, 160, FEATS), BF16),
             pltpu.VMEM((count, 160, FEATS), BF16),
-            pltpu.VMEM((nz, CHUNK, 128), F32),
-            pltpu.VMEM((nz, CHUNK, 128), F32),
-            pltpu.VMEM((plane, CHUNK, 128), F32),
+            pltpu.VMEM((nz, plane, QUAD, 128), F32),
+            pltpu.VMEM((nz, plane, QUAD, 128), F32),
+            pltpu.VMEM((plane, QUAD, 128), F32),
+            pltpu.VMEM((plane, QUAD, 128), F32),
             dma((2,)),
             dma((2, 3)),
             dma((2, 3)),
@@ -632,6 +677,8 @@
             dma((nz,)),
             dma((plane,)),
             dma((plane,)),
+            dma((plane,)),
+            dma((plane,)),
             dma((nz,)),
             dma((nz,)),
         ],

time: 121 us -> 107 us (0.88)
  local copies, waits for them, and re-layouts: 11.5 us -> 6.37 us
  Pallas kernels: 103 us -> 98.3 us
  other arithmetic: 4.96 us -> 1.8 us
    pallas_call x1, Pallas kernels: 103 us -> 98.3 us  [whole_call(): pl.pallas_call(whole_kernel, in_specs=[anywhere] * 2 + [inside] * len(con...]
    slice x2 -> x0, local copies, waits for them, and re-layouts: 1.79 us -> none  [the longest x1 0.96 us: whole_call(): w_back = jnp.concatenate([w_qkv[:, 0:96], gap, w_k, gap, w_v, gap], 1)]
    add x1 -> x0, other arithmetic: 1.74 us -> none  [whole_call(): b_kv = jnp.asarray(key_features()) + b_row[None, :]]
    concatenate x3 -> x0, other arithmetic: 1.46 us -> none  [the longest x1 0.71 us: whole_call(): w_kv = jnp.concatenate([w_k, gap, w_v, gap], 1)]
    pad x1 -> x0, local copies, waits for them, and re-layouts: 1.41 us -> none  [whole_call(): table = jnp.pad(table, ((0, 5), (0, SPREAD - TABLE)))]
    unnamed x2 -> x1, local copies, waits for them, and re-layouts: 3.67 us -> 2.67 us
where the time goes in v3:
time: 107 us
  Pallas kernels  98.3 us (92%)
  local copies, waits for them, and re-layouts  6.37 us (6%)
  other arithmetic  1.8 us (2%)
    pallas_call x1, Pallas kernels, whole_call(): pl.pallas_call(whole_kernel, in_specs=[anywhere] * 2 + [inside] * len(con...  98.3 us
    unnamed x1, local copies, waits for them, and re-layouts  2.67 us

profile of v3, /device:TPU:0, one launch (start us, length us, event | category | flops | bytes accessed | tf_op | source)
XLA Modules:
  0.0 107.1 jit_solution(10480555476773697260)
XLA Ops:
  0.6 1.2 %broadcast_in_dim.11.b_raw_ref = f32[1,288]{1,0:T(1,128)} reshape(f32[288]{0:T(512)} %param.16) | data formatting | bytes 2304 | tf_op jit(solution)/shard_map/broadcast_in_dim | solution.py:616
  1.9 98.3 %shard_map.162 = (bf16[28,28,7,96]{3,2,1,0:T(8,128)(2,1)}, f32[8,16,4,128]{3,2,1,0:T(4,128)}) custom-call(bf16[28,28,7,96]{3,2,1,0:T(8,128)(2,1)} %x_hbm.1, bf16[28,28,7,96]{3,2,1,0:T(8,128)(2,1)} %dy_hbm.1, f32[1,96]{1,0:T(1,128)} %bitcast.13, f32[1,96]{1,0:T(1,128)} %bitcast.14, f32[3,2197]{1,0:T(4,128)} %table_ref.1, ...), custom_call_target="tpu_custom_call" | custom-call | tf_op jit(solution)/shard_map/pallas_call | solution.py:625
  100.2 1.0 broadcast_multiply_fusion
  101.2 0.6 fusion
  101.9 0.8 pad_maximum_fusion
  102.6 0.5 slice_bitcast_fusion
  103.2 0.6 reshape.24
  103.8 0.7 reshape.23
  104.5 2.7 %copy.19 = bf16[28,28,7,96]{3,2,1,0:T(8,128)(2,1)} copy(bf16[28,28,7,96]{3,2,1,0:T(8,128)(2,1)} %get-tuple-element.24) | data formatting | bytes 2107392
  (2 shorter events, 0.0 us)

commit v4 on v3

--- a/solution.py
+++ b/solution.py
@@ -23,8 +23,8 @@
 SQUEEZED = 768
 OWN = 196
 OTHER = 147
-AHEAD = 3
-LAG = 2
+AHEAD = 4
+LAG = 3
 QUAD = 4
 MESH = pl.DeviceIdType.MESH
 FAR = -(2.0**100)
@@ -276,7 +276,7 @@
         return pltpu.make_async_remote_copy(
             src_ref=fwd_send_ref.at[t],
             dst_ref=fwd_recv_ref.at[t],
-            send_sem=fwd_send.at[t],
+            send_sem=fwd_send,
             recv_sem=fwd_recv.at[t],
             device_id=peer_z(nz - 1),
             device_id_type=MESH,
@@ -286,7 +286,7 @@
         return pltpu.make_async_remote_copy(
             src_ref=ret_send_ref.at[t],
             dst_ref=ret_recv_ref.at[t],
-            send_sem=ret_send.at[t],
+            send_sem=ret_send,
             recv_sem=ret_recv.at[t],
             device_id=peer_z(1),
             device_id_type=MESH,
@@ -307,19 +307,21 @@
             device_id_type=MESH,
         )
 
-    def store_out():
-        inner_x = pl.ds(SHIFT, cells_x - SHIFT)
+    def store_out(n):
+        first, last = ((SHIFT, 17), (24, cells_x), (17, 24))[n]
+        rows = pl.ds(first, last - first)
         inner_y = pl.ds(SHIFT, cells_y - SHIFT)
-        return pltpu.make_async_copy(
-            out_ext_ref.at[inner_x, inner_y], out_hbm.at[inner_x, inner_y], out_sem
-        )
+        return pltpu.make_async_copy(out_ext_ref.at[rows, inner_y], out_hbm.at[rows, inner_y], out_sem.at[n])
+
+    def wait_bytes(like, sem):
+        pltpu.make_async_copy(like, like, sem).wait()
 
     def near(k):
         return pltpu.make_async_remote_copy(
             src_ref=pay_ref.at[lax.rem(gz + k, nz)],
             dst_ref=near_ref.at[gz],
-            send_sem=near_send.at[k],
-            recv_sem=near_recv.at[k],
+            send_sem=near_send,
+            recv_sem=near_recv,
             device_id=peer_z(k),
             device_id_type=MESH,
         )
@@ -328,8 +330,8 @@
         return pltpu.make_async_remote_copy(
             src_ref=part_ref.at[lax.rem(spot + k, plane)],
             dst_ref=far_ref.at[spot],
-            send_sem=far_send.at[k],
-            recv_sem=far_recv.at[k],
+            send_sem=far_send,
+            recv_sem=far_recv,
             device_id=peer_xy(k),
             device_id_type=MESH,
         )
@@ -338,8 +340,8 @@
         return pltpu.make_async_remote_copy(
             src_ref=result_ref.at[gz, spot],
             dst_ref=result_ref.at[gz, spot],
-            send_sem=share_send.at[k],
-            recv_sem=share_recv.at[k],
+            send_sem=share_send,
+            recv_sem=share_recv,
             device_id=peer_xy(k),
             device_id_type=MESH,
         )
@@ -348,8 +350,8 @@
         return pltpu.make_async_remote_copy(
             src_ref=result_ref.at[gz],
             dst_ref=result_ref.at[gz],
-            send_sem=all_send.at[k],
-            recv_sem=all_recv.at[k],
+            send_sem=all_send,
+            recv_sem=all_recv,
             device_id=peer_z(k),
             device_id_type=MESH,
         )
@@ -555,14 +557,10 @@
         def _():
             near(k).start()
 
-    def last_merge(t, carry):
-        merge(t)
-        return carry
-
-    lax.fori_loop(total - LAG, total, last_merge, 0)
-    store_out().start()
     for side in range(3):
         edge(side).start()
+    store_out(0).start()
+    store_out(1).start()
     for n in range(5):
         put(438 + n, jnp.sum(rows_ref[n], 0, keepdims=True))
     fold_table(acc_ref, ones_ref, wide_ref, flat_ref, put)
@@ -571,41 +569,41 @@
         def _():
             near(k).start()
     near_ref[gz] = pay_ref[gz]
-    for k in range(1, nz):
-        near(k).wait_recv()
+
+    def last_merge(t, carry):
+        merge(t)
+        return carry
+
+    lax.fori_loop(total - LAG, total, last_merge, 0)
+    store_out(2).start()
+    most_z = pl.ds(0, nz - 1)
+    most_xy = pl.ds(0, plane - 1)
+    wait_bytes(near_ref.at[most_z], near_recv)
     part_ref[...] = jnp.sum(near_ref[...], 0)
     for k in range(1, plane):
         far(k).start()
     far_ref[spot] = part_ref[spot]
-    for k in range(1, plane):
-        far(k).wait_recv()
+    wait_bytes(far_ref.at[most_xy], far_recv)
     result_ref[gz, spot] = jnp.sum(far_ref[...], 0)
     for k in range(1, plane):
         share(k).start()
-    for k in range(1, plane):
-        share(k).wait_recv()
+    wait_bytes(far_ref.at[most_xy], share_recv)
     for k in range(1, nz):
         final(k).start()
-    store_out().wait()
+    for n in range(3):
+        store_out(n).wait()
     for side in range(3):
         edge(side).wait()
     for a in range(2):
         for side in range(3):
             halo(a, side).wait_send()
-
-    def drain(t, carry):
-        fwd(t).wait_send()
-        ret(t).wait_send()
-        return carry
-
-    lax.fori_loop(0, total, drain, 0)
-    for k in range(1, nz):
-        near(k).wait_send()
-    for k in range(1, plane):
-        far(k).wait_send()
-        share(k).wait_send()
-    for k in range(1, nz):
-        final(k).wait()
+    wait_bytes(fwd_send_ref, fwd_send)
+    wait_bytes(ret_send_ref, ret_send)
+    wait_bytes(near_ref.at[most_z], near_send)
+    wait_bytes(far_ref.at[most_xy], far_send)
+    wait_bytes(far_ref.at[most_xy], share_send)
+    wait_bytes(near_ref.at[most_z], all_send)
+    wait_bytes(near_ref.at[most_z], all_recv)
 
 
 def whole_call(inputs, d_out, gain, shift, table, w_qkv, b_qkv, w_proj):
@@ -666,21 +664,21 @@
             dma((2,)),
             dma((2, 3)),
             dma((2, 3)),
+            dma,
             dma((count,)),
+            dma,
             dma((count,)),
-            dma((count,)),
-            dma((count,)),
-            dma,
             dma((3,)),
             dma((3,)),
-            dma((nz,)),
-            dma((nz,)),
-            dma((plane,)),
-            dma((plane,)),
-            dma((plane,)),
-            dma((plane,)),
-            dma((nz,)),
-            dma((nz,)),
+            dma((3,)),
+            dma,
+            dma,
+            dma,
+            dma,
+            dma,
+            dma,
+            dma,
+            dma,
         ],
         compiler_params=pltpu.CompilerParams(
             vmem_limit_bytes=56 << 20, collective_id=0, has_side_effects=True

time: 107 us -> 100 us (0.935)
  Pallas kernels: 98.3 us -> 91.4 us
    pallas_call x1, Pallas kernels: 98.3 us -> 91.4 us  [whole_call(): pl.pallas_call(whole_kernel, in_specs=[anywhere] * 2 + [inside] * len(con...]
where the time goes in v4:
time: 100 us
  Pallas kernels  91.4 us (91%)
  local copies, waits for them, and re-layouts  6.37 us (6%)
  other arithmetic  1.8 us (2%)
    pallas_call x1, Pallas kernels, whole_call(): pl.pallas_call(whole_kernel, in_specs=[anywhere] * 2 + [inside] * len(con...  91.4 us
    unnamed x1, local copies, waits for them, and re-layouts  2.67 us

profile of v4, /device:TPU:0, one launch (start us, length us, event | category | flops | bytes accessed | tf_op | source)
XLA Modules:
  0.0 100.2 jit_solution(10376197911340358793)
XLA Ops:
  0.6 1.2 %broadcast_in_dim.11.b_raw_ref = f32[1,288]{1,0:T(1,128)} reshape(f32[288]{0:T(512)} %param.16) | data formatting | bytes 2304 | tf_op jit(solution)/shard_map/broadcast_in_dim | solution.py:614
  1.9 91.4 %shard_map.162 = (bf16[28,28,7,96]{3,2,1,0:T(8,128)(2,1)}, f32[8,16,4,128]{3,2,1,0:T(4,128)}) custom-call(bf16[28,28,7,96]{3,2,1,0:T(8,128)(2,1)} %x_hbm.1, bf16[28,28,7,96]{3,2,1,0:T(8,128)(2,1)} %dy_hbm.1, f32[1,96]{1,0:T(1,128)} %bitcast.13, f32[1,96]{1,0:T(1,128)} %bitcast.14, f32[3,2197]{1,0:T(4,128)} %table_ref.1, ...), custom_call_target="tpu_custom_call" | custom-call | tf_op jit(solution)/shard_map/pallas_call | solution.py:623
  93.2 1.0 %broadcast_multiply_fusion = f32[8,16,4,128]{3,2,1,0:T(4,128)S(1)} fusion(f32[8,16,4,128]{3,2,1,0:T(4,128)} %get-tuple-element.10), kind=kLoop, calls=%fused_computation.1 | loop fusion | flops 65536 | bytes 524288 | tf_op jit(solution)/shard_map/mul | solution.py:692
  94.3 0.6 fusion
  94.9 0.8 pad_maximum_fusion
  95.7 0.5 slice_bitcast_fusion
  96.2 0.6 reshape.24
  96.8 0.7 reshape.23
  97.5 2.7 %copy.19 = bf16[28,28,7,96]{3,2,1,0:T(8,128)(2,1)} copy(bf16[28,28,7,96]{3,2,1,0:T(8,128)(2,1)} %get-tuple-element.24) | data formatting | bytes 2107392
  (2 shorter events, 0.0 us)

commit v5 on v4

--- a/solution.py
+++ b/solution.py
@@ -24,6 +24,7 @@
 OWN = 196
 OTHER = 147
 AHEAD = 4
+FIRST = 8
 LAG = 3
 QUAD = 4
 MESH = pl.DeviceIdType.MESH
@@ -154,11 +155,11 @@
 
 
 def window_at(t):
-    inner = jnp.where(t < 5, t, t - 7)
-    edge = t - 5
+    inner = jnp.where(t < FIRST, t, t - 7)
+    edge = t - FIRST
     side_x = jnp.where(edge < 4, 3, edge - 4)
     side_y = jnp.where(edge < 4, edge, 3)
-    is_edge = (t >= 5) & (t < 12)
+    is_edge = (t >= FIRST) & (t < FIRST + 7)
     return jnp.where(is_edge, side_x, inner // 3), jnp.where(is_edge, side_y, inner % 3)
 
 
@@ -308,7 +309,7 @@
         )
 
     def store_out(n):
-        first, last = ((SHIFT, 17), (24, cells_x), (17, 24))[n]
+        first, last = ((SHIFT, 10), (24, cells_x), (10, 24))[n]
         rows = pl.ds(first, last - first)
         inner_y = pl.ds(SHIFT, cells_y - SHIFT)
         return pltpu.make_async_copy(out_ext_ref.at[rows, inner_y], out_hbm.at[rows, inner_y], out_sem.at[n])
@@ -517,7 +518,7 @@
                 out_ext_ref[wx * WIN + SHIFT + ix, wy * WIN + SHIFT + iy] = tile[0:7]
 
     def step(t, carry):
-        @pl.when(t == 5 - AHEAD)
+        @pl.when(t == FIRST - AHEAD)
         def _():
             for a in range(2):
                 for side in range(3):
@@ -557,8 +558,8 @@
         def _():
             near(k).start()
 
-    for side in range(3):
-        edge(side).start()
+    edge(0).start()
+    edge(2).start()
     store_out(0).start()
     store_out(1).start()
     for n in range(5):
@@ -575,6 +576,7 @@
         return carry
 
     lax.fori_loop(total - LAG, total, last_merge, 0)
+    edge(1).start()
     store_out(2).start()
     most_z = pl.ds(0, nz - 1)
     most_xy = pl.ds(0, plane - 1)

time: 100 us -> 102 us (1.020)
  Pallas kernels: 91.4 us -> 93.1 us
    pallas_call x1, Pallas kernels: 91.4 us -> 93.1 us  [whole_call(): pl.pallas_call(whole_kernel, in_specs=[anywhere] * 2 + [inside] * len(con...]
where the time goes in v5:
time: 102 us
  Pallas kernels  93.1 us (91%)
  local copies, waits for them, and re-layouts  6.37 us (6%)
  other arithmetic  1.8 us (2%)
    pallas_call x1, Pallas kernels, whole_call(): pl.pallas_call(whole_kernel, in_specs=[anywhere] * 2 + [inside] * len(con...  93.1 us
    unnamed x1, local copies, waits for them, and re-layouts  2.67 us

profile of v5, /device:TPU:0, one launch (start us, length us, event | category | flops | bytes accessed | tf_op | source)
XLA Modules:
  0.0 101.9 jit_solution(12364090933772965973)
XLA Ops:
  0.6 1.2 %broadcast_in_dim.11.b_raw_ref = f32[1,288]{1,0:T(1,128)} reshape(f32[288]{0:T(512)} %param.16) | data formatting | bytes 2304 | tf_op jit(solution)/shard_map/broadcast_in_dim | solution.py:616
  1.9 93.1 %shard_map.162 = (bf16[28,28,7,96]{3,2,1,0:T(8,128)(2,1)}, f32[8,16,4,128]{3,2,1,0:T(4,128)}) custom-call(bf16[28,28,7,96]{3,2,1,0:T(8,128)(2,1)} %x_hbm.1, bf16[28,28,7,96]{3,2,1,0:T(8,128)(2,1)} %dy_hbm.1, f32[1,96]{1,0:T(1,128)} %bitcast.13, f32[1,96]{1,0:T(1,128)} %bitcast.14, f32[3,2197]{1,0:T(4,128)} %table_ref.1, ...), custom_call_target="tpu_custom_call" | custom-call | tf_op jit(solution)/shard_map/pallas_call | solution.py:625
  95.0 1.0 %broadcast_multiply_fusion = f32[8,16,4,128]{3,2,1,0:T(4,128)S(1)} fusion(f32[8,16,4,128]{3,2,1,0:T(4,128)} %get-tuple-element.10), kind=kLoop, calls=%fused_computation.1 | loop fusion | flops 65536 | bytes 524288 | tf_op jit(solution)/shard_map/mul | solution.py:694
  96.0 0.6 fusion
  96.6 0.8 pad_maximum_fusion
  97.4 0.5 slice_bitcast_fusion
  97.9 0.6 reshape.24
  98.6 0.7 reshape.23
  99.2 2.7 %copy.19 = bf16[28,28,7,96]{3,2,1,0:T(8,128)(2,1)} copy(bf16[28,28,7,96]{3,2,1,0:T(8,128)(2,1)} %get-tuple-element.24) | data formatting | bytes 2107392
  (2 shorter events, 0.0 us)

commit v6 on v4

--- a/solution.py
+++ b/solution.py
@@ -137,7 +137,7 @@
             flat_ref[at : at + 8, 0:LANES] = jnp.where(sub < WIN, own, 0.0)
             flat_ref[at : at + 8, LANES:SQUEEZED] = jnp.where(sub < WIN, other, 0.0)
     spread = None
-    for piece in pieces(flat_ref[...], 3):
+    for piece in pieces(flat_ref[...], 2):
         part = nt(piece, ones_ref[...])
         spread = part if spread is None else spread + part
     wide_ref[0] = spread
@@ -163,6 +163,7 @@
 
 
 def whole_kernel(
+    factor,
     x_hbm,
     dy_hbm,
     gain_ref,
@@ -584,7 +585,7 @@
         far(k).start()
     far_ref[spot] = part_ref[spot]
     wait_bytes(far_ref.at[most_xy], far_recv)
-    result_ref[gz, spot] = jnp.sum(far_ref[...], 0)
+    result_ref[gz, spot] = jnp.sum(far_ref[...], 0) * factor
     for k in range(1, plane):
         share(k).start()
     wait_bytes(far_ref.at[most_xy], share_recv)
@@ -606,7 +607,7 @@
     wait_bytes(near_ref.at[most_z], all_recv)
 
 
-def whole_call(inputs, d_out, gain, shift, table, w_qkv, b_qkv, w_proj):
+def whole_call(factor, inputs, d_out, gain, shift, table, w_qkv, b_qkv, w_proj):
     cells_x, cells_y, cells_z, _ = inputs.shape
     count = (cells_x // WIN) * (cells_y // WIN)
     nz, plane = lax.axis_size("gz"), lax.axis_size("gx") * lax.axis_size("gy")
@@ -621,7 +622,7 @@
     inside = pl.BlockSpec(memory_space=pltpu.VMEM)
     dma = pltpu.SemaphoreType.DMA
     return pl.pallas_call(
-        whole_kernel,
+        functools.partial(whole_kernel, factor),
         in_specs=[anywhere] * 2 + [inside] * len(consts),
         out_specs=[anywhere, inside],
         out_shape=outs,
@@ -687,9 +688,10 @@
 
 
 def shards(inputs, d_out, gain, shift, w_qkv, b_qkv, w_proj, rel_bias):
-    field, sums = whole_call(inputs, d_out, gain, shift, rel_bias, w_qkv, b_qkv, w_proj)
     count = inputs.size // FEATS * lax.axis_size("gx") * lax.axis_size("gy") * lax.axis_size("gz")
-    sums = sums.reshape(-1, 128) * float(count) ** -0.5
+    factor = float(count) ** -0.5
+    field, sums = whole_call(factor, inputs, d_out, gain, shift, rel_bias, w_qkv, b_qkv, w_proj)
+    sums = sums.reshape(-1, 128)
     weight = jnp.concatenate([sums[0:96, :96], sums[96:192, :96], sums[192:288, :96]], 1)
     proj = sums[288:384, :96]
     rel = sums[384:438].reshape(HEADS, SPREAD)[:, :TABLE]

time: 100 us -> 102 us (1.020)
  local copies, waits for them, and re-layouts: 6.37 us -> 9.43 us
  other arithmetic: 1.8 us -> 0.78 us
where the time goes in v6:
time: 102 us
  Pallas kernels  90.7 us (89%)
  local copies, waits for them, and re-layouts  9.43 us (9%)
    pallas_call x1, Pallas kernels, whole_call(): pl.pallas_call(functools.partial(whole_kernel, factor), in_specs=[anywher...  90.7 us
    unnamed x1, local copies, waits for them, and re-layouts  2.67 us

profile of v6, /device:TPU:0, one launch (start us, length us, event | category | flops | bytes accessed | tf_op | source)
XLA Modules:
  0.0 101.5 jit_solution(13697852551853164072)
XLA Ops:
  0.6 1.2 %broadcast_in_dim.11.b_raw_ref = f32[1,288]{1,0:T(1,128)} reshape(f32[288]{0:T(512)} %param.16) | data formatting | bytes 2304 | tf_op jit(solution)/shard_map/broadcast_in_dim | solution.py:615
  1.9 90.7 %shard_map.162 = (bf16[28,28,7,96]{3,2,1,0:T(8,128)(2,1)}, f32[8,16,4,128]{3,2,1,0:T(4,128)}) custom-call(bf16[28,28,7,96]{3,2,1,0:T(8,128)(2,1)} %x_hbm.1, bf16[28,28,7,96]{3,2,1,0:T(8,128)(2,1)} %dy_hbm.1, f32[1,96]{1,0:T(1,128)} %bitcast.13, f32[1,96]{1,0:T(1,128)} %bitcast.14, f32[3,2197]{1,0:T(4,128)} %table_ref.1, ...), custom_call_target="tpu_custom_call" | custom-call | tf_op jit(solution)/shard_map/pallas_call | solution.py:624
  92.6 1.5 %fusion = (f32[96,96]{1,0:T(8,128)}, f32[96,96]{1,0:T(8,128)S(1)}, f32[96,96]{1,0:T(8,128)S(1)}, f32[96,96]{1,0:T(8,128)S(1)}) fusion(f32[512,128]{1,0:T(8,128)} %bitcast.8), kind=kLoop, calls=%fused_computation.3 | loop fusion | bytes 294912 | tf_op jit(solution)/shard_map/slice | solution.py:696
  94.1 0.8 pad_maximum_fusion
  94.9 1.3 %slice_bitcast_fusion = (f32[96]{0:T(128)}, f32[96]{0:T(128)}) fusion(f32[512,128]{1,0:T(8,128)} %bitcast.9), kind=kLoop, calls=%fused_computation.1 | loop fusion | bytes 1536 | tf_op jit(solution)/shard_map/squeeze | solution.py:699
  96.1 0.8 slice.41
  96.9 0.6 reshape.25
  97.5 0.7 slice.39
  98.2 0.7 reshape.24
  98.9 2.7 %copy.19 = bf16[28,28,7,96]{3,2,1,0:T(8,128)(2,1)} copy(bf16[28,28,7,96]{3,2,1,0:T(8,128)(2,1)} %get-tuple-element.24) | data formatting | bytes 2107392
